TPU v7x, 128 devices: a whole 4x4x4 slice. The times are simulated.
128 devices in a mesh: gx: 8 (over z, y_hi), gy: 16 (over x, y_lo, core).
Axes of the slice: x: 4, y: 4 (y_hi: 2, y_lo: 2; y = y_hi * 2 + y_lo), z: 4, core: 2. Of those that a mesh axis runs over, the one named last changes fastest.
Arguments:
- interior_inverse: bfloat16 [16, 16, 1536, 1536], P('gx', 'gy'), as said below
- coupling: bfloat16 [16, 16, 1536, 1024], P('gx', 'gy'), may hold values from -0.15625 to 0.15625
- face_stiffness: bfloat16 [16, 16, 4, 256, 256], P('gx', 'gy'), as said below
- corner_basis: bfloat16 [16, 16, 24, 1024], P('gx', 'gy'), may hold values from -0.25 to 0.25
- loads: float32 [16, 16, 4, 256], P('gx', 'gy'), may hold values from -48 to 48
- face_order: int32 [16, 16, 4, 256], P('gx', 'gy'), may hold values from 0 to 255, each once within a row
- corner_index: int32 [16, 16, 24], P('gx', 'gy'), may hold values from 0 to 1791, as said below
- coarse_inverse: float32 [1792, 1792], P(None, ('gx', 'gy')), as said below
Outputs:
- solution: float32 [16, 16, 4, 256], P('gx', 'gy')
- residual: float32 [16, 16, 4, 256], P('gx', 'gy')
Inputs may be any that keep to these rules, and one draw needn't show every extreme that they name: `interior_inverse`: symmetric positive definite. `face_stiffness`: each block is symmetric, and every subdomain's interface Schur complement is positive definite. `corner_index`: subdomains that share a grid vertex give its 6 coarse dofs the same indices in the same order (corners in the order top-left, top-right, bottom-left, bottom-right); the 24 indices of a subdomain are distinct; distinct vertices have distinct indices. `coarse_inverse`: symmetric positive definite.
All inputs are finite; a program needn't handle non-finite values.
Results may differ from a plain program's by a relative error of at most 0.01.
Values sent between devices are 32-bit elements; how exact they have to be, the bound alone decides.
No kernel may reach another device: no remote copies, remote signals or barrier semaphores. Data moves between devices by JAX's collectives and lax.ppermute only.
A program may use at most 128 MiB of HBM per device.

v0:
```python
import jax
import jax.numpy as jnp
from jax import lax
from jax.sharding import Mesh
from jax.sharding import PartitionSpec as P

ITERS = 2
GX = ("gx_0", "gx_1")
GY = ("gy_0", "gy_1", "gy_2")
GX_GY = ("gx_0", "gx_1", "gy_0", "gy_1", "gy_2")


careful = lax.Precision.HIGHEST


def from_behind(value, axis, steps):
    count = lax.axis_size(axis)
    first, last = (max(0, -steps), min(count, count - steps))
    return lax.ppermute(value, axis, [(source, source + steps) for source in range(first, last)])


def by_axis(array, axes):
    for axis in axes:
        array = lax.psum(array, axis)
    return array


def inverse_order(ordering):
    extent = ordering.shape[-1]
    levels = jnp.arange(extent, dtype=jnp.int32)
    matches = ordering[..., :, None] == levels
    return jnp.sum(jnp.where(matches, levels[:, None], 0), axis=-2)


def reorder(values, positions):
    return jnp.take_along_axis(values, positions, axis=-1)


def permute_block(matrix, ordering):
    extent = ordering.shape[-1]
    levels = jnp.arange(extent, dtype=jnp.int32)
    picker = (ordering[..., None, :] == levels[:, None]).astype(jnp.float32)
    rows_done = jnp.einsum("sfgk,sfkl->sfgl", picker, matrix, precision=careful)
    return jnp.einsum("sfgl,sfhl->sfgh", rows_done, picker, precision=careful)


def invert(summed):
    factor_low = jnp.linalg.cholesky(summed)
    identity = jnp.broadcast_to(jnp.eye(summed.shape[-1], dtype=jnp.float32), summed.shape)
    factor = lax.linalg.triangular_solve(factor_low, identity, left_side=True, lower=True)
    return jnp.einsum("...ik,...il->...kl", factor, factor, precision=careful)


def half_inner(first, second):
    return 0.5 * jnp.sum(first * second)


def swap_vectors(vector_in):
    from_above = from_behind(vector_in[-1, 1], GX, 1)
    from_below = from_behind(vector_in[0, 0], GX, -1)
    from_west = from_behind(vector_in[:, 3], GY, 1)
    from_east = from_behind(vector_in[:, 2], GY, -1)
    north_side = jnp.concatenate([from_above[None], vector_in[:-1, 1]], axis=0)
    south_side = jnp.concatenate([vector_in[1:, 0], from_below[None]], axis=0)
    return jnp.stack([north_side, south_side, from_west, from_east], axis=1)


def shards(
    interior_inverse,
    coupling,
    face_stiffness,
    corner_basis,
    loads,
    face_order,
    corner_index,
    coarse_inverse,
):
    local_count = interior_inverse.shape[0]
    inner_dofs = interior_inverse.shape[2]
    face_dofs = loads.shape[3]
    inverse_mat = interior_inverse.reshape(local_count, inner_dofs, inner_dofs)
    couple = coupling.reshape(local_count, inner_dofs, 4 * face_dofs)
    couple_faces = couple.reshape(local_count, inner_dofs, 4, face_dofs)
    stiffness = face_stiffness.reshape(local_count, 4, face_dofs, face_dofs)
    basis = corner_basis.reshape(local_count, corner_basis.shape[2], 4 * face_dofs)
    basis_wide = basis.astype(jnp.float32)
    ordering = face_order.reshape(local_count, 4, face_dofs)
    backward = inverse_order(ordering)
    corners = corner_index.reshape(local_count, corner_index.shape[2])
    coarse_total = coarse_inverse.shape[0]
    row_ids = lax.axis_index(GX) * local_count + jnp.arange(local_count, dtype=jnp.int32)
    col_id = lax.axis_index(GY)
    row_total = local_count * lax.axis_size(GX)
    col_total = lax.axis_size(GY)
    west_live = jnp.broadcast_to(col_id > 0, (local_count,))
    east_live = jnp.broadcast_to(col_id < col_total - 1, (local_count,))
    live_mask = jnp.stack(
        [row_ids > 0, row_ids < row_total - 1, west_live, east_live], axis=1
    ).astype(jnp.float32)[:, :, None]
    products = jnp.einsum(
        "sij,sjk->sik", inverse_mat, couple, preferred_element_type=jnp.float32
    ).astype(jnp.bfloat16)
    product_faces = products.reshape(local_count, inner_dofs, 4, face_dofs)
    schur_local = stiffness.astype(jnp.float32) - jnp.einsum(
        "sifk,sifl->sfkl", couple_faces, product_faces, preferred_element_type=jnp.float32
    )
    schur_canon = permute_block(schur_local, ordering)
    partner = from_behind(schur_canon[0, 0], GX, -1)
    partner_south = jnp.concatenate([schur_canon[1:, 0], partner[None]], axis=0)
    partner_side = from_behind(schur_canon[:, 2], GY, -1)
    south_inverse = invert(schur_canon[:, 1] + partner_south)
    east_inverse = invert(schur_canon[:, 3] + partner_side)
    top_inverse = from_behind(south_inverse[-1], GX, 1)
    north_inverse = jnp.concatenate([top_inverse[None], south_inverse[:-1]], axis=0)
    west_inverse = from_behind(east_inverse, GY, 1)
    face_inverse = jnp.stack([north_inverse, south_inverse, west_inverse, east_inverse], axis=1)
    loads_canon = reorder(loads.reshape(local_count, 4, face_dofs), backward)
    residual = live_mask * (loads_canon + swap_vectors(loads_canon))
    solution = jnp.zeros_like(residual)
    search = jnp.zeros_like(residual)
    along = jnp.zeros_like(residual)
    gamma_old = jnp.float32(1.0)
    alpha_old = jnp.float32(1.0)
    for iteration in range(ITERS):
        smoothed = jnp.einsum("sfkl,sfl->sfk", face_inverse, residual, precision=careful)
        share = jnp.einsum("sfkl,sfl->sfk", schur_canon, smoothed, precision=careful)
        share_local = (
            reorder(share, ordering).astype(jnp.bfloat16).reshape(local_count, 4 * face_dofs)
        )
        corner_res = jnp.einsum(
            "sjk,sk->sj", basis, share_local, preferred_element_type=jnp.float32
        )
        matches = (corners[:, :, None] == jnp.arange(coarse_total, dtype=jnp.int32)).astype(
            jnp.float32
        )
        dense = jnp.einsum("sj,sjg->g", corner_res, matches, precision=careful)
        owned = lax.psum_scatter(dense, GX_GY, scatter_dimension=0, tiled=True)
        partial_sol = jnp.dot(coarse_inverse, owned, precision=careful)
        coarse_sol = by_axis(partial_sol, GX_GY)
        corner_sol = jnp.einsum("sjg,g->sj", matches, coarse_sol, precision=careful)
        lifted = jnp.einsum("sjk,sj->sk", basis_wide, corner_sol, precision=careful).reshape(
            local_count, 4, face_dofs
        )
        spread = jnp.einsum(
            "sfkl,sfl->sfk", schur_canon, reorder(lifted, backward), precision=careful
        )
        precond_out = live_mask * jnp.einsum(
            "sfkl,sfl->sfk",
            face_inverse,
            residual + spread + swap_vectors(spread),
            precision=careful,
        )
        plain = reorder(precond_out, ordering).astype(jnp.bfloat16)
        middle = jnp.einsum(
            "sik,sk->si",
            couple,
            plain.reshape(local_count, 4 * face_dofs),
            preferred_element_type=jnp.float32,
        ).astype(jnp.bfloat16)
        solved = jnp.einsum(
            "sij,sj->si", inverse_mat, middle, preferred_element_type=jnp.float32
        ).astype(jnp.bfloat16)
        direct = jnp.einsum("sfkl,sfl->sfk", stiffness, plain, preferred_element_type=jnp.float32)
        back_part = jnp.einsum(
            "sifk,si->sfk", couple_faces, solved, preferred_element_type=jnp.float32
        )
        canon_out = reorder(direct - back_part, backward)
        image = live_mask * (canon_out + swap_vectors(canon_out))
        gamma, delta = (
            by_axis(half_inner(residual, precond_out), GX_GY),
            by_axis(half_inner(precond_out, image), GX_GY),
        )
        if iteration == 0:
            alpha = gamma / delta
            search = precond_out
            along = image
        else:
            beta = gamma / gamma_old
            alpha = gamma / (delta - beta * gamma / alpha_old)
            search = precond_out + beta * search
            along = image + beta * along
        solution = solution + alpha * search
        residual = residual - alpha * along
        gamma_old = gamma
        alpha_old = alpha
    return (
        solution.reshape(local_count, 1, 4, face_dofs),
        residual.reshape(local_count, 1, 4, face_dofs),
    )


def solution(mesh):
    torus = Mesh(mesh.devices.reshape(4, 2, 4, 2, 2), ("gx_0", "gx_1", "gy_0", "gy_1", "gy_2"))
    in_specs = (
        P(GX, GY, None, None),
        P(GX, GY, None, None),
        P(GX, GY, None, None, None),
        P(GX, GY, None, None),
        P(GX, GY, None, None),
        P(GX, GY, None, None),
        P(GX, GY, None),
        P(None, GX_GY),
    )
    out_specs = (P(GX, GY, None, None), P(GX, GY, None, None))
    return jax.shard_map(
        shards, mesh=torus, in_specs=in_specs, out_specs=out_specs, check_vma=False
    )
```

profile of v0, /device:TPU:1, one launch (start us, length us, event | category | flops | bytes accessed | tf_op | source)
XLA Modules:
  0.0 947.1 jit_solution(5315609379234085832)
XLA Ops:
  0.6 11.2 %reshape_reshape.3 = bf16[2,1536,4,256]{3,2,1,0:T(4,128)(2,1)} reshape(bf16[2,1,1536,1024]{3,2,1,0:T(8,128)(2,1)} %param.14) | data formatting | bytes 12582912 | tf_op jit(solution)/shard_map/reshape;reshape | solution.py:83
  11.9 16.5 %fusion.11 = bf16[2,1536,1024]{1,2,0:T(8,128)(2,1)} fusion(bf16[2,1,1536,1024]{3,2,1,0:T(8,128)(2,1)} %param.14, bf16[2,1,1536,1536]{3,2,1,0:T(8,128)(2,1)} %param.13), kind=kOutput, calls=%fused_computation.24 | convolution fusion | flops 9666822144 | bytes 22020096 | tf_op jit(solution)/shard_map/sij,sjk->sik/dot_general | solution.py:100
  28.9 6.4 fusion.20
  44.6 3.3 collective-permute-start.6
  48.4 20.4 %gather_fusion = f32[2048]{0:T(1024)S(1)} fusion(f32[2,4,256]{2,1,0:T(4,128)S(1)} %bitcast.383, s32[2048]{0:T(1024)S(1)} %bitcast.390), kind=kCustom, calls=%fused_computation.clone | custom fusion | bytes 40960 | tf_op jit(solution)/shard_map/jit(take_along_axis)/gather | solution.py:36
  70.1 6.3 collective-permute-start
  78.2 3.9 collective-permute-start.2
  103.6 23.5 %custom-call.36 = f32[2,128,128]{2,1,0:T(8,128)S(1)} custom-call(f32[2,128,128]{2,1,0:T(8,128)S(1)} %cholesky.198), custom_call_target="Cholesky" | custom-call | tf_op jit(solution)/shard_map/jit(cholesky)/cholesky | solution.py:48
  134.8 24.3 %custom-call.40 = f32[2,128,128]{2,1,0:T(8,128)S(1)} custom-call(f32[2,128,128]{2,1,0:T(8,128)} %cholesky.201), custom_call_target="Cholesky" | custom-call | tf_op jit(solution)/shard_map/jit(cholesky)/cholesky | solution.py:48
  160.5 21.1 %custom-call.37 = f32[2,1,128,128]{2,3,1,0:T(8,128)} custom-call(f32[2,1,128,128]{3,2,1,0:T(8,128)} %get-tuple-element.99), custom_call_target="InvertDiagBlocksLowerTriangular" | custom-call | tf_op jit(solution)/shard_map/jit(cholesky)/cholesky | solution.py:48
  185.4 25.0 %custom-call.38 = f32[2,128,128]{2,1,0:T(8,128)} custom-call(f32[2,128,128]{2,1,0:T(8,128)} %convolution_subtract_fusion.2), custom_call_target="Cholesky" | custom-call | tf_op jit(solution)/shard_map/jit(cholesky)/cholesky | solution.py:48
  210.5 21.1 %custom-call.41 = f32[2,1,128,128]{2,3,1,0:T(8,128)} custom-call(f32[2,1,128,128]{3,2,1,0:T(8,128)} %get-tuple-element.100), custom_call_target="InvertDiagBlocksLowerTriangular" | custom-call | tf_op jit(solution)/shard_map/jit(cholesky)/cholesky | solution.py:48
  236.2 24.9 %custom-call.42 = f32[2,128,128]{2,1,0:T(8,128)} custom-call(f32[2,128,128]{2,1,0:T(8,128)} %slice_subtract_fusion), custom_call_target="Cholesky" | custom-call | tf_op jit(solution)/shard_map/jit(cholesky)/cholesky | solution.py:48
  267.1 8.7 while.4
  268.4 3.1 bitcast_dynamic-update-slice_fusion.4
  272.8 3.0 bitcast_dynamic-update-slice_fusion.4
  275.8 40.9 %custom-call.39 = f32[2,2,128,128]{2,3,1,0:T(8,128)} custom-call(f32[2,2,128,128]{3,2,1,0:T(8,128)} %bitcast.412), custom_call_target="InvertDiagBlocksLowerTriangular" | custom-call | tf_op jit(solution)/shard_map/triangular_solve/custom-call.0 | solution.py:50
  323.3 8.7 while.5
  324.7 3.1 bitcast_dynamic-update-slice_fusion.5
  329.1 3.0 bitcast_dynamic-update-slice_fusion.5
  332.1 40.7 %custom-call.43 = f32[2,2,128,128]{2,3,1,0:T(8,128)} custom-call(f32[2,2,128,128]{3,2,1,0:T(8,128)} %bitcast.411), custom_call_target="InvertDiagBlocksLowerTriangular" | custom-call | tf_op jit(solution)/shard_map/triangular_solve/custom-call.0 | solution.py:50
  378.0 3.6 collective-permute-start.7
  381.7 6.4 collective-permute-start.5
  390.1 3.3 collective-permute-done.5
  397.3 21.2 %gather_fusion.1 = bf16[2048]{0:T(1024)(128)(2,1)S(1)} fusion(bf16[2,4,256]{2,1,0:T(4,128)(2,1)S(1)} %bitcast.384, s32[2048]{0:T(1024)S(1)} %bitcast.386), kind=kCustom, calls=%fused_computation.1.clone | custom fusion | bytes 32768 | tf_op jit(solution)/shard_map/jit(take_along_axis)/gather | solution.py:36
  419.0 73.2 %all-reduce.1 = f32[1792]{0:T(1024)S(1)} all-reduce(f32[1792]{0:T(1024)S(1)} %convolution_reduce_fusion.3), channel_id=2, replica_groups=mesh['gx_0'=4,'gx_1'=2,'gy_0'=4,'gy_1'=2,'gy_2'=2] {'gx_0','gx_1','gy_0'..., use_global_device_ids=true, to_apply=%region_5.0.clone | all-reduce | flops 1792 | bytes 14336
  492.5 7.6 psum.210
  500.1 5.4 psum.211
  505.4 7.3 psum.212
  512.7 3.8 psum.213
  516.6 9.1 psum.214
  526.5 20.4 %gather_fusion.2 = f32[2048]{0:T(1024)S(1)} fusion(f32[2,4,256]{2,1,0:T(4,128)S(1)} %reshape.122, s32[2048]{0:T(1024)S(1)} %bitcast.393), kind=kCustom, calls=%fused_computation.2.clone | custom fusion | bytes 40960 | tf_op jit(solution)/shard_map/jit(take_along_axis)/gather | solution.py:36
  553.0 3.6 collective-permute-start.10
  558.6 2.9 collective-permute-done.11
  563.5 20.4 %gather_fusion.3 = bf16[2048]{0:T(1024)(128)(2,1)S(1)} fusion(f32[2,4,256]{2,1,0:T(4,128)S(1)} %bitcast_multiply_fusion.1, s32[2048]{0:T(1024)S(1)} %bitcast.387), kind=kCustom, calls=%fused_computation.3.clone | custom fusion | bytes 32768 | tf_op jit(solution)/shard_map/jit(take_along_axis)/gather | solution.py:36
  583.9 4.7 fusion.8
  588.6 6.4 fusion.2
  596.4 20.4 %gather_fusion.4 = f32[2048]{0:T(1024)S(1)} fusion(f32[2,4,256]{2,1,0:T(4,128)S(1)} %bitcast_subtract_fusion.3, s32[2048]{0:T(1024)S(1)} %bitcast.391), kind=kCustom, calls=%fused_computation.4.clone | custom fusion | bytes 40960 | tf_op jit(solution)/shard_map/jit(take_along_axis)/gather | solution.py:36
  616.8 6.4 collective-permute-start.12
  633.4 10.4 %all-reduce.6 = (f32[]{:T(128)}, f32[]{:T(128)}) all-reduce(f32[]{:T(128)S(6)} %mul.109, f32[]{:T(128)S(6)} %mul.112), channel_id=1, replica_groups=mesh['gx_0'=4,'gx_1'=2,'gy_0'=4,'gy_1'=2,'gy_2'=2] {'gx_0'}, use_global_device_ids=true, to_apply=%region_12.0 | all-reduce | flops 2 | bytes 16 | tf_op jit(solution)/shard_map/psum | solution.py:24
  643.8 5.9 all-reduce.12
  649.7 7.2 all-reduce.4
  656.8 6.0 all-reduce.10
  662.9 8.7 all-reduce.8
  673.0 3.4 fusion.27
  678.2 20.8 %gather_fusion.5 = bf16[2048]{0:T(1024)(128)(2,1)S(1)} fusion(bf16[2,4,256]{2,1,0:T(4,128)(2,1)S(1)} %bitcast.385, s32[2048]{0:T(1024)S(1)} %bitcast.388), kind=kCustom, calls=%fused_computation.5.clone | custom fusion | bytes 32768 | tf_op jit(solution)/shard_map/jit(take_along_axis)/gather | solution.py:36
  699.5 61.9 %all-reduce.2 = f32[1792]{0:T(1024)S(1)} all-reduce(f32[1792]{0:T(1024)S(1)} %convolution_reduce_fusion.2), channel_id=3, replica_groups=mesh['gx_0'=4,'gx_1'=2,'gy_0'=4,'gy_1'=2,'gy_2'=2] {'gx_0','gx_1','gy_0'..., use_global_device_ids=true, to_apply=%region_23.0.clone | all-reduce | flops 1792 | bytes 14336
  761.7 7.9 psum.225
  769.6 5.4 psum.226
  774.9 7.0 psum.227
  781.9 3.8 psum.228
  785.7 9.1 psum.229
  795.7 20.4 %gather_fusion.6 = f32[2048]{0:T(1024)S(1)} fusion(f32[2,4,256]{2,1,0:T(4,128)S(1)} %reshape.125, s32[2048]{0:T(1024)S(1)} %bitcast.394), kind=kCustom, calls=%fused_computation.6.clone | custom fusion | bytes 40960 | tf_op jit(solution)/shard_map/jit(take_along_axis)/gather | solution.py:36
  821.9 3.3 collective-permute-start.18
  832.1 20.4 %gather_fusion.7 = bf16[2048]{0:T(1024)(128)(2,1)S(1)} fusion(f32[2,4,256]{2,1,0:T(4,128)S(1)} %bitcast_multiply_fusion, s32[2048]{0:T(1024)S(1)} %bitcast.389), kind=kCustom, calls=%fused_computation.7.clone | custom fusion | bytes 32768 | tf_op jit(solution)/shard_map/jit(take_along_axis)/gather | solution.py:36
  852.5 4.7 fusion.6
  857.2 6.4 fusion
  864.9 20.4 %gather_fusion.8 = f32[2048]{0:T(1024)S(1)} fusion(f32[2,4,256]{2,1,0:T(4,128)S(1)} %bitcast_subtract_fusion.2, s32[2048]{0:T(1024)S(1)} %bitcast.392), kind=kCustom, calls=%fused_computation.8.clone | custom fusion | bytes 40960 | tf_op jit(solution)/shard_map/jit(take_along_axis)/gather | solution.py:36
  885.4 6.4 collective-permute-start.20
  902.1 10.9 %all-reduce.5 = (f32[]{:T(128)}, f32[]{:T(128)}) all-reduce(f32[]{:T(128)S(6)} %mul.118, f32[]{:T(128)S(6)} %mul.121), channel_id=1, replica_groups=mesh['gx_0'=4,'gx_1'=2,'gy_0'=4,'gy_1'=2,'gy_2'=2] {'gx_0'}, use_global_device_ids=true, to_apply=%region_30.0 | all-reduce | flops 2 | bytes 16 | tf_op jit(solution)/shard_map/psum | solution.py:24
  913.0 6.0 all-reduce.11
  918.9 7.9 all-reduce.3
  926.8 5.3 all-reduce.9
  932.1 8.8 all-reduce.7
  (292 shorter events, 130.5 us)
Async XLA Ops:
  0.6 491.6 %copy-start = (f32[1792,14]{0,1:T(8,128)S(1)}, f32[1792,14]{0,1:T(8,128)}, u32[]{:S(2)}) copy-start(f32[1792,14]{0,1:T(8,128)} %param.20) | copy-start | bytes 301060
  11.9 16.5 %copy-start.2 = (bf16[2,1,4,256,256]{4,3,2,1,0:T(8,128)(2,1)S(1)}, bf16[2,1,4,256,256]{4,3,2,1,0:T(8,128)(2,1)}, u32[]{:S(2)}) copy-start(bf16[2,1,4,256,256]{4,3,2,1,0:T(8,128)(2,1)} %param.15) | copy-start | bytes 3145732
  28.9 6.4 copy-start.17
  39.9 8.5 copy-start.1
  39.9 57.4 %collective-permute-start.4 = (f32[256,256]{0,1:T(8,128)}, f32[256,256]{0,1:T(8,128)}, u32[]{:S(2)}, u32[]{:S(2)}) collective-permute-start(f32[256,256]{0,1:T(8,128)} %bitcast.410), channel_id=1, source_target_pairs={{16,0},{32,16},{48,32},{64,48},{80,64},{96,80},{112,96},{17,1},{33... | collective-permute-start | bytes 786440 | tf_op jit(solution)/shard_map/ppermute | solution.py:19
  44.6 83.3 %collective-permute-start.6 = (f32[2,256,256]{1,2,0:T(8,128)}, f32[2,256,256]{1,2,0:T(8,128)}, u32[]{:S(2)}, u32[]{:S(2)}) collective-permute-start(f32[2,256,256]{1,2,0:T(8,128)} %bitcast.409), channel_id=1, source_target_pairs={{1,0},{2,1},{3,2},{4,3},{5,4},{6,5},{7,6},{8,7},{9,8},{10,9},{11,1... | collective-permute-start | bytes 1572872 | tf_op jit(solution)/shard_map/ppermute | solution.py:19
  48.3 20.5 %copy-start.19 = (s32[2,4,256]{2,1,0:T(4,128)}, s32[2,4,256]{2,1,0:T(4,128)S(1)}, u32[]{:S(2)}) copy-start(s32[2,4,256]{2,1,0:T(4,128)S(1)} %select_reduce_fusion) | copy-start | bytes 24580
  70.1 24.0 %collective-permute-start = (f32[256]{0:T(256)}, f32[256]{0:T(256)}, u32[]{:S(2)}, u32[]{:S(2)}) collective-permute-start(f32[256]{0:T(256)} %bitcast.3), channel_id=1, source_target_pairs={{0,16},{16,32},{32,48},{48,64},{64,80},{80,96},{96,112},{1,17},{17... | collective-permute-start | bytes 3080 | tf_op jit(solution)/shard_map/ppermute | solution.py:19
  76.3 311.7 %collective-permute-start.1 = (f32[256]{0:T(256)}, f32[256]{0:T(256)}, u32[]{:S(2)}, u32[]{:S(2)}) collective-permute-start(f32[256]{0:T(256)} %bitcast.7), channel_id=1, source_target_pairs={{16,0},{32,16},{48,32},{64,48},{80,64},{96,80},{112,96},{17,1},{33... | collective-permute-start | bytes 3080 | tf_op jit(solution)/shard_map/ppermute | solution.py:19
  78.2 310.5 %collective-permute-start.2 = (f32[2,256]{1,0:T(2,128)}, f32[2,256]{1,0:T(2,128)}, u32[]{:S(2)}, u32[]{:S(2)}) collective-permute-start(f32[2,256]{1,0:T(2,128)} %get-tuple-element.129), channel_id=1, source_target_pairs={{0,1},{1,2},{2,3},{3,4},{4,5},{5,6},{6,7},{7,8},{8,9},{9,10},{10,1... | collective-permute-start | bytes 6152 | tf_op jit(solution)/shard_map/ppermute | solution.py:19
  84.1 9.3 copy-start.24
  94.1 295.3 %collective-permute-start.3 = (f32[2,256]{1,0:T(2,128)}, f32[2,256]{1,0:T(2,128)}, u32[]{:S(2)}, u32[]{:S(2)}) collective-permute-start(f32[2,256]{1,0:T(2,128)} %get-tuple-element.130), channel_id=1, source_target_pairs={{1,0},{2,1},{3,2},{4,3},{5,4},{6,5},{7,6},{8,7},{9,8},{10,9},{11,1... | collective-permute-start | bytes 6152 | tf_op jit(solution)/shard_map/ppermute | solution.py:19
  102.8 0.8 copy-start.7
  133.3 0.8 copy-start.6
  261.1 4.6 copy-start.31
  262.9 53.8 %copy-start.9 = (f32[128,256]{1,0:T(8,128)S(1)}, f32[128,256]{1,0:T(8,128)}, u32[]{:S(2)}) copy-start(f32[128,256]{1,0:T(8,128)} %get-tuple-element.94) | copy-start | bytes 393220
  263.2 54.8 %copy-start.8 = (f32[128,256]{1,0:T(8,128)S(1)}, f32[128,256]{1,0:T(8,128)}, u32[]{:S(2)}) copy-start(f32[128,256]{1,0:T(8,128)} %get-tuple-element.93) | copy-start | bytes 393220
  372.8 8.8 copy-start.3
  372.8 15.2 %copy-start.26 = (f32[1,256]{1,0:T(1,128)S(1)}, f32[1,256]{1,0:T(1,128)}, u32[]{:S(2)}) copy-start(f32[1,256]{1,0:T(1,128)} %get-tuple-element.127) | copy-start | bytes 3076
  372.8 15.9 %copy-start.25 = (f32[2,256]{1,0:T(2,128)S(1)}, f32[2,256]{1,0:T(2,128)}, u32[]{:S(2)}) copy-start(f32[2,256]{1,0:T(2,128)} %pad_maximum_fusion.1) | copy-start | bytes 6148
  372.8 17.2 %copy-start.21 = (f32[2,4]{1,0:T(2,128)S(1)}, f32[2,4]{1,0:T(2,128)}, u32[]{:S(2)}) copy-start(f32[2,4]{1,0:T(2,128)} %add_convert_fusion) | copy-start | bytes 100
  378.0 17.4 %copy-start.10 = (f32[2,256,256]{2,1,0:T(8,128)}, f32[2,256,256]{2,1,0:T(8,128)S(1)}, u32[]{:S(2)}) copy-start(f32[2,256,256]{2,1,0:T(8,128)S(1)} %fusion.44) | copy-start | bytes 1572868
  378.0 15.5 %collective-permute-start.7 = (f32[2,256,256]{2,1,0:T(8,128)S(1)}, f32[2,256,256]{2,1,0:T(8,128)S(1)}, u32[]{:S(2)}, u32[]{:S(2)}) collective-permute-start(f32[2,256,256]{2,1,0:T(8,128)S(1)} %fusion.44), channel_id=1, source_target_pairs={{0,1},{1,2},{2,3},{3,4},{4,5},{5,6},{6,7},{7,8},{8,9},{9,10},{10,1... | collective-permute-start | bytes 1572872 | tf_op jit(solution)/shard_map/ppermute | solution.py:19
  381.7 11.8 %collective-permute-start.5 = (f32[256,256]{1,0:T(8,128)S(1)}, f32[256,256]{1,0:T(8,128)S(1)}, u32[]{:S(2)}, u32[]{:S(2)}) collective-permute-start(f32[256,256]{1,0:T(8,128)S(1)} %get-tuple-element.91), channel_id=1, source_target_pairs={{0,16},{16,32},{32,48},{48,64},{64,80},{80,96},{96,112},{1,17},{17... | collective-permute-start | bytes 786440 | tf_op jit(solution)/shard_map/ppermute | solution.py:19
  393.5 1.9 copy-start.13
  393.5 1.9 copy-start.27
  397.2 21.2 %copy-start.18 = (s32[2,1,4,256]{3,2,1,0:T(4,128)S(1)}, s32[2,1,4,256]{3,2,1,0:T(4,128)}, u32[]{:S(2)}) copy-start(s32[2,1,4,256]{3,2,1,0:T(4,128)} %param.18) | copy-start | bytes 24580
  397.3 21.3 %copy-start.16 = (bf16[2,1,24,1024]{3,2,1,0:T(8,128)(2,1)S(1)}, bf16[2,1,24,1024]{3,2,1,0:T(8,128)(2,1)}, u32[]{:S(2)}) copy-start(bf16[2,1,24,1024]{3,2,1,0:T(8,128)(2,1)} %param.16) | copy-start | bytes 294916
  397.3 21.4 %copy-start.30 = (s32[2,1,24]{2,1,0:T(1,128)S(1)}, s32[2,1,24]{2,1,0:T(1,128)}, u32[]{:S(2)}) copy-start(s32[2,1,24]{2,1,0:T(1,128)} %param.19) | copy-start | bytes 580
  526.5 20.5 %copy-start.20 = (s32[2,4,256]{2,1,0:T(4,128)S(1)}, s32[2,4,256]{2,1,0:T(4,128)}, u32[]{:S(2)}) copy-start(s32[2,4,256]{2,1,0:T(4,128)} %copy-done.19) | copy-start | bytes 24580
  546.9 14.6 %copy-start.22 = (f32[2,4]{1,0:T(2,128)S(1)}, f32[2,4]{1,0:T(2,128)}, u32[]{:S(2)}) copy-start(f32[2,4]{1,0:T(2,128)} %add_convert_fusion) | copy-start | bytes 100
  547.0 14.6 %copy-start.4 = (f32[2,256,256]{2,1,0:T(8,128)S(1)}, f32[2,256,256]{2,1,0:T(8,128)}, u32[]{:S(2)}) copy-start(f32[2,256,256]{2,1,0:T(8,128)} %fusion.40) | copy-start | bytes 1572868
  547.0 14.6 %copy-start.11 = (f32[2,256,256]{2,1,0:T(8,128)S(1)}, f32[2,256,256]{2,1,0:T(8,128)}, u32[]{:S(2)}) copy-start(f32[2,256,256]{2,1,0:T(8,128)} %copy-done.10) | copy-start | bytes 1572868
  547.0 14.6 %copy-start.14 = (f32[2,1,256,256]{3,2,0,1:T(8,128)S(1)}, f32[2,1,256,256]{3,2,0,1:T(8,128)}, u32[]{:S(2)}) copy-start(f32[2,1,256,256]{3,2,0,1:T(8,128)} %copy-done.13) | copy-start | bytes 1572868
  547.0 14.6 %copy-start.28 = (f32[2,256,256]{2,1,0:T(8,128)S(1)}, f32[2,256,256]{2,1,0:T(8,128)}, u32[]{:S(2)}) copy-start(f32[2,256,256]{2,1,0:T(8,128)} %copy-done.27) | copy-start | bytes 1572868
  548.9 9.6 %collective-permute-start.8 = (f32[256]{0:T(256)S(1)}, f32[256]{0:T(256)S(1)}, u32[]{:S(2)}, u32[]{:S(2)}) collective-permute-start(f32[256]{0:T(256)S(1)} %bitcast.451), channel_id=1, source_target_pairs={{0,16},{16,32},{32,48},{48,64},{64,80},{80,96},{96,112},{1,17},{17... | collective-permute-start | bytes 3080 | tf_op jit(solution)/shard_map/ppermute | solution.py:19
  551.7 6.8 collective-permute-start.9
  553.0 5.6 collective-permute-start.10
  556.6 4.9 collective-permute-start.11
  583.9 11.1 %slice-start = ((s8[6291456]{0:T(1024)(128)(4,1)}), s8[4194304]{0:T(1024)(128)(4,1)S(1)}, s32[]{:S(2)}) async-start(s8[6291456]{0:T(1024)(128)(4,1)} %bitcast.395), calls=%async_computation | async-start | bytes 8388608
  588.6 6.4 slice-start.1
  596.4 20.5 %copy-start.23 = (pred[2,4,256]{2,0,1:T(4,128)(4,1)S(1)}, pred[2,4,256]{2,0,1:T(4,128)(4,1)}, u32[]{:S(2)}) copy-start(pred[2,4,256]{2,0,1:T(4,128)(4,1)} %get-tuple-element.81) | copy-start | bytes 6148
  616.8 12.0 %collective-permute-start.12 = (f32[256]{0:T(256)S(1)}, f32[256]{0:T(256)S(1)}, u32[]{:S(2)}, u32[]{:S(2)}) collective-permute-start(f32[256]{0:T(256)S(1)} %bitcast.452), channel_id=1, source_target_pairs={{0,16},{16,32},{32,48},{48,64},{64,80},{80,96},{96,112},{1,17},{17... | collective-permute-start | bytes 3080 | tf_op jit(solution)/shard_map/ppermute | solution.py:19
  623.2 5.8 collective-permute-start.13
  624.5 4.5 collective-permute-start.14
  626.5 4.9 collective-permute-start.15
  816.1 14.0 %copy-start.5 = (f32[2,256,256]{2,1,0:T(8,128)S(1)}, f32[2,256,256]{2,1,0:T(8,128)}, u32[]{:S(2)}) copy-start(f32[2,256,256]{2,1,0:T(8,128)} %fusion.40) | copy-start | bytes 1572868
  816.1 14.0 %copy-start.12 = (f32[2,256,256]{2,1,0:T(8,128)S(1)}, f32[2,256,256]{2,1,0:T(8,128)}, u32[]{:S(2)}) copy-start(f32[2,256,256]{2,1,0:T(8,128)} %copy-done.10) | copy-start | bytes 1572868
  816.1 14.0 %copy-start.15 = (f32[2,1,256,256]{3,2,0,1:T(8,128)S(1)}, f32[2,1,256,256]{3,2,0,1:T(8,128)}, u32[]{:S(2)}) copy-start(f32[2,1,256,256]{3,2,0,1:T(8,128)} %copy-done.13) | copy-start | bytes 1572868
  816.2 14.0 %copy-start.29 = (f32[2,256,256]{2,1,0:T(8,128)S(1)}, f32[2,256,256]{2,1,0:T(8,128)}, u32[]{:S(2)}) copy-start(f32[2,256,256]{2,1,0:T(8,128)} %copy-done.27) | copy-start | bytes 1572868
  818.1 9.3 collective-permute-start.16
  820.6 6.8 collective-permute-start.17
  821.9 5.6 collective-permute-start.18
  825.2 4.9 collective-permute-start.19
  852.5 11.1 %slice-start.2 = ((s8[6291456]{0:T(1024)(128)(4,1)}), s8[4194304]{0:T(1024)(128)(4,1)S(1)}, s32[]{:S(2)}) async-start(s8[6291456]{0:T(1024)(128)(4,1)} %bitcast.397), calls=%async_computation.2 | async-start | bytes 8388608
  857.2 6.4 slice-start.3
  885.4 12.0 %collective-permute-start.20 = (f32[256]{0:T(256)S(1)}, f32[256]{0:T(256)S(1)}, u32[]{:S(2)}, u32[]{:S(2)}) collective-permute-start(f32[256]{0:T(256)S(1)} %bitcast.454), channel_id=1, source_target_pairs={{0,16},{16,32},{32,48},{48,64},{64,80},{80,96},{96,112},{1,17},{17... | collective-permute-start | bytes 3080 | tf_op jit(solution)/shard_map/ppermute | solution.py:19
  891.8 5.8 collective-permute-start.21
  893.1 4.5 collective-permute-start.22
  895.1 5.0 collective-permute-start.23
where the time goes:
time: 958 us; the launch traced here: 947 us
  blocking collectives  278 us (29%)
  other arithmetic  246 us (26%)
  local copies, waits for them, and re-layouts  239 us (25%)
  matrix products  88.5 us (9%)
  starting transfers between devices  70.9 us (7%)
  waiting for transfers between devices  13.9 us (1%)
  between operations  10.7 us (1%)
    gather x19, local copies, waits for them, and re-layouts, reorder(): return jnp.take_along_axis(values, positions, axis=-1)  185 us
    another operation x14, other arithmetic, invert(): factor_low = jnp.linalg.cholesky(summed)  145 us
    psum x20, blocking collectives, by_axis(): array = lax.psum(array, axis)  143 us
    unnamed x2, blocking collectives  135 us
    another operation x5, other arithmetic, invert(): lax.linalg.triangular_solve(factor_low, identity, left_side=True, lower=T...  85.3 us
    ppermute x24, starting transfers between devices, from_behind(): lax.ppermute(value, axis, [(source, source + steps) for source in range(f...  70.9 us
    another operation x16, local copies, waits for them, and re-layouts, invert(): lax.linalg.triangular_solve(factor_low, identity, left_side=True, lower=T...  20.3 us
  transfers between devices with their start and end apart: 24, of which 7 were waited for; matrix products, arithmetic and copies ran while one was open for 34% of the time, Pallas kernels for 0%

commit v1 on v0

v1 whole, which is shorter than its diff:
```python
import jax
import jax.numpy as jnp
from jax import lax
from jax.experimental import pallas as pl
from jax.experimental.pallas import tpu as pltpu
from jax.sharding import Mesh
from jax.sharding import PartitionSpec as P

GX = ("gx_0", "gx_1")
GY = ("gy_0", "gy_1", "gy_2")
GX_GY = GX + GY

NI = 1536
NF = 256
NCOR = 24
NCOARSE = 1792
OWN = 14
GRID_X = 8
GRID_Y = 16
DEV = 128
PKT = 288
STEPS = 3
CHUNK = NI // STEPS
VC = 24
F32 = jnp.float32
BF16 = jnp.bfloat16
HIGHEST = lax.Precision.HIGHEST

FACE = ((0, 1, 3, 5), (1, 2, 4, 6))
GROUPS = ((0, 2), (0, 1), (1, 3), (0, 4), (1, 5), (0, 6), (1, 7))
GROUP_ROW = (0, 1, -1, 2, 0, 1, 0, 1)
GROUP_COL = (1, 1, 1, 1, 0, 0, 2, 2)


def nn(a, b):
    return lax.dot_general(a, b, (((1,), (0,)), ((), ())), preferred_element_type=F32)


def nt(a, b):
    return lax.dot_general(a, b, (((1,), (1,)), ((), ())), preferred_element_type=F32)


def split2(x):
    hi = x.astype(BF16)
    return hi, (x - hi.astype(F32)).astype(BF16)


def split3(x):
    hi = x.astype(BF16)
    rest = x - hi.astype(F32)
    mid = rest.astype(BF16)
    return hi, mid, (rest - mid.astype(F32)).astype(BF16)


def iota(shape, dim):
    return lax.broadcasted_iota(jnp.int32, shape, dim)


def schur_kernel(order, inverse, couple, stiff, basis, loads, index, s_out, p_in, p_n, p_s, p_w, p_e, ct, prod, pick):
    sub = pl.program_id(0)
    step = pl.program_id(1)

    @pl.when(step == 0)
    def _():
        for f in range(4):
            chosen = (iota((NF, NF), 0) == order[f : f + 1, :]).astype(BF16)
            pick[f] = chosen
            ct[f * NF : (f + 1) * NF, :] = nt(chosen, couple[:, f * NF : (f + 1) * NF]).astype(BF16)

    prod[pl.ds(step * CHUNK, CHUNK), :] = nt(inverse[...], ct[...]).astype(BF16)

    @pl.when(step == STEPS - 1)
    def _():
        for f in range(4):
            rows = slice(f * NF, (f + 1) * NF)
            back = nn(ct[rows, :], prod[:, f * NF :])
            chosen = pick[f]
            canon = nt(nn(chosen, stiff[f]).astype(BF16), chosen)
            diag = canon - back[:, :NF]
            s_out[rows, rows] = diag
            if f < 3:
                s_out[rows, (f + 1) * NF :] = -back[:, NF:]
            lowered = nt(basis[:, f * NF : (f + 1) * NF], chosen).astype(BF16)
            hi, lo = split2(diag)
            corner = nn(lowered, hi) + nn(lowered, lo)
            parts = jnp.concatenate(
                [part.astype(F32) for part in split3(jnp.broadcast_to(loads[f : f + 1, :], (8, NF)))], axis=0
            ).astype(BF16)
            placed = nt(parts, chosen)
            load = placed[0:8] + placed[8:16] + placed[16:24]
            tail = jnp.where(iota((8, NF), 0) == 0, load, jnp.broadcast_to(index[...], (8, NF)))

            def put(out, lead):
                out[lead + (slice(0, NF), slice(None))] = diag
                out[lead + (slice(NF, NF + NCOR), slice(None))] = corner
                out[lead + (slice(NF + NCOR, NF + NCOR + 8), slice(None))] = tail

            if f == 0:
                pl.when(sub == 0)(lambda: put(p_n, ()))
                pl.when(sub == 1)(lambda: put(p_in, (1,)))
            elif f == 1:
                pl.when(sub == 0)(lambda: put(p_in, (0,)))
                pl.when(sub == 1)(lambda: put(p_s, ()))
            elif f == 2:
                put(p_w, ())
            else:
                put(p_e, ())


def schur(order, inverse, couple, stiff, basis, loads, index):
    pkt = jax.ShapeDtypeStruct((PKT, NF), F32)
    pair = jax.ShapeDtypeStruct((2, PKT, NF), F32)
    return pl.pallas_call(
        schur_kernel,
        grid=(2, STEPS),
        in_specs=[
            pl.BlockSpec((None, None, 4, NF), lambda s, j: (s, 0, 0, 0)),
            pl.BlockSpec((None, None, CHUNK, NI), lambda s, j: (s, 0, j, 0)),
            pl.BlockSpec((None, None, NI, 4 * NF), lambda s, j: (s, 0, 0, 0)),
            pl.BlockSpec((None, None, 4, NF, NF), lambda s, j: (s, 0, 0, 0, 0)),
            pl.BlockSpec((None, None, NCOR, 4 * NF), lambda s, j: (s, 0, 0, 0)),
            pl.BlockSpec((None, None, 4, NF), lambda s, j: (s, 0, 0, 0)),
            pl.BlockSpec((None, 1, NF), lambda s, j: (s, 0, 0)),
        ],
        out_specs=[
            pl.BlockSpec((None, 4 * NF, 4 * NF), lambda s, j: (s, 0, 0)),
            pl.BlockSpec((2, PKT, NF), lambda s, j: (0, 0, 0)),
            pl.BlockSpec((PKT, NF), lambda s, j: (0, 0)),
            pl.BlockSpec((PKT, NF), lambda s, j: (0, 0)),
            pl.BlockSpec((None, PKT, NF), lambda s, j: (s, 0, 0)),
            pl.BlockSpec((None, PKT, NF), lambda s, j: (s, 0, 0)),
        ],
        out_shape=[jax.ShapeDtypeStruct((2, 4 * NF, 4 * NF), F32), pair, pkt, pkt, pair, pair],
        scratch_shapes=[
            pltpu.VMEM((4 * NF, NI), BF16),
            pltpu.VMEM((NI, 4 * NF), BF16),
            pltpu.VMEM((4, NF, NF), BF16),
        ],
        compiler_params=pltpu.CompilerParams(
            dimension_semantics=("arbitrary", "arbitrary"), vmem_limit_bytes=56 * 2**20
        ),
        cost_estimate=pl.CostEstimate(flops=16 * 10**9, transcendentals=0, bytes_accessed=32 * 2**20),
        name="schur",
    )(order, inverse, couple, stiff, basis, loads, index)


def vertex_kernel(table, columns, out):
    total = jnp.zeros((GRID_Y, 2, 128), F32)
    for ix in range(GRID_X):
        total = total + table[ix * GRID_Y : (ix + 1) * GRID_Y]
    hi, mid, lo = split3(columns[...])
    lhs = jnp.concatenate([hi, mid, lo], axis=0)
    rows = iota((NCOARSE, 256), 0) + 1
    last = total[GRID_Y - 1, 1:2, :]
    for pair in range(9):
        first = total[2 * pair, 0:1, :] if pair < 8 else last
        second = total[2 * pair + 1, 0:1, :] if pair < 8 else jnp.zeros((1, 128), F32)
        wanted = jnp.concatenate([first, second], axis=1).astype(jnp.int32)
        chosen = (rows == wanted).astype(BF16)
        got = nn(lhs, chosen)
        got = got[0:16] + got[16:32] + got[32:48]
        out[2 * pair + 1] = got[:, :128]
        if pair < 8:
            out[2 * pair + 2] = got[:, 128:]
    for other in (0, *range(18, VC)):
        out[other] = jnp.zeros((16, 128), F32)


def vertex_order(table, columns):
    return pl.pallas_call(
        vertex_kernel,
        out_shape=jax.ShapeDtypeStruct((VC, 16, 128), F32),
        compiler_params=pltpu.CompilerParams(vmem_limit_bytes=40 * 2**20),
        cost_estimate=pl.CostEstimate(flops=10**9, transcendentals=0, bytes_accessed=2**20),
        name="vertex_order",
    )(table, columns)


def spread_window(place, contributions):
    corner = iota((NCOR, 128), 0)
    lane = iota((NCOR, 128), 1)
    below = jnp.where(corner >= 12, 1, 0)
    inside = corner - 12 * below
    right = inside >= 6
    dof = inside - jnp.where(right, 6, 0)
    cols = [jnp.zeros((1, 128), F32) for _ in range(4)]
    for g, value in contributions.items():
        target = (2 * place[0] + GROUP_ROW[g] + below) * 6 + dof
        filled = jnp.where(lane == target, jnp.broadcast_to(value, (NCOR, 128)), 0.0)
        left = jnp.sum(jnp.where(right, 0.0, filled), axis=0, keepdims=True)
        both = jnp.sum(filled, axis=0, keepdims=True)
        cols[GROUP_COL[g]] = cols[GROUP_COL[g]] + left
        cols[GROUP_COL[g] + 1] = cols[GROUP_COL[g] + 1] + (both - left)
    return cols


def row_dot(matrix, row):
    return jnp.sum(matrix * row, axis=1, keepdims=True)


def face_kernel(place, live, p_in, p_n, p_s, p_w, p_e, q_n, q_s, q_w, q_e, finv, tmap, r_out, z_out, slots, send, a_hi, a_lo, x):
    def pieces(m):
        if m == 0:
            return p_n, (), q_n, (), live[0]
        if m == 1:
            return p_in, (0,), p_in, (1,), 1.0
        if m == 2:
            return p_s, (), q_s, (), live[1]
        if m < 5:
            return p_w, (m - 3,), q_w, (m - 3,), live[2]
        return p_e, (m - 5,), q_e, (m - 5,), live[3]

    eye = jnp.where(iota((NF, NF), 0) == iota((NF, NF), 1), 1.0, 0.0)
    guess = []
    for m in range(7):
        own, at, other, there, _ = pieces(m)
        full = own[at + (slice(0, NF), slice(None))] + other[there + (slice(0, NF), slice(None))]
        hi, lo = split2(full)
        a_hi[m] = hi
        a_lo[m] = lo
        size = jnp.max(jnp.sum(jnp.abs(full), axis=0, keepdims=True))
        scale = 1.9 / size
        guess.append(scale)
        x[m] = scale * (2.0 * eye - scale * full)

    def rough(state):
        count, _ = state
        worst = jnp.float32(0.0)
        for m in range(7):
            now = x[m]
            near = now.astype(BF16)
            left = eye - nn(a_hi[m], near)
            worst = jnp.maximum(worst, jnp.sum(left * left))
            x[m] = now + nn(near, left.astype(BF16))
        return count + 1, worst

    def rough_on(state):
        count, worst = state
        return jnp.logical_and(count < 24, jnp.logical_not(worst < 0.1))

    _, worst = lax.while_loop(rough_on, rough, (jnp.int32(0), jnp.float32(1e9)))
    fine_start = worst < 0.1

    @pl.when(jnp.logical_not(fine_start))
    def _():
        for m in range(7):
            x[m] = guess[m] * eye

    def fine(state):
        count, _ = state
        worst = jnp.float32(0.0)
        for m in range(7):
            now = x[m]
            hi, lo = split2(now)
            left = eye - (nn(a_hi[m], hi) + (nn(a_hi[m], lo) + nn(a_lo[m], hi)))
            worst = jnp.maximum(worst, jnp.sum(left * left))
            x[m] = now + nn(hi, left.astype(BF16))
        return count + 1, worst

    def fine_on(state):
        count, worst = state
        return jnp.logical_and(count < 60, jnp.logical_not(worst < 1e-4))

    lax.while_loop(fine_on, fine, (jnp.int32(0), jnp.float32(1e9)))

    gathered = {}

    def gather(g, value):
        gathered[g] = value if g not in gathered else gathered[g] + value

    rows_r = []
    rows_z = []
    rows_i = [None] * 8
    for m in range(7):
        own, at, other, there, alive = pieces(m)
        inverse = x[m] * alive
        finv[m] = inverse
        both = jnp.concatenate(
            [own[at + (slice(NF, NF + NCOR), slice(None))], other[there + (slice(NF, NF + NCOR), slice(None))]], axis=0
        )
        b_hi, b_lo = split2(both)
        i_hi, i_lo = split2(inverse)
        lifted = nn(jnp.concatenate([b_hi, b_lo], axis=0), i_hi)
        mapped = lifted[:48] + lifted[48:] + nn(b_hi, i_lo)
        tmap[m] = mapped
        line = slice(NF + NCOR, NF + NCOR + 1)
        resid = alive * (own[at + (line, slice(None))] + other[there + (line, slice(None))])
        rows_r.append(resid)
        resid_hi, resid_mid, resid_lo = split3(jnp.broadcast_to(resid, (8, NF)))
        rows_z.append(resid)
        gather(GROUPS[m][0], row_dot(mapped[:NCOR], resid))
        if m == 1:
            gather(GROUPS[m][1], row_dot(mapped[NCOR:], resid))
        tail = slice(NF + NCOR + 1, NF + NCOR + 2)
        rows_i[GROUPS[m][0]] = own[at + (tail, slice(0, 128))]
        rows_i[GROUPS[m][1]] = other[there + (tail, slice(0, 128))]
    resid = jnp.concatenate(rows_r + [jnp.zeros((1, NF), F32)], axis=0)
    r_out[...] = resid
    z_out[...] = face_apply(finv, resid)
    slots[...] = jnp.transpose(jnp.concatenate(rows_i, axis=0))[:NCOR, :]
    window = jnp.concatenate(spread_window(place, gathered), axis=0)
    send[...] = jnp.broadcast_to(window[None], (DEV, 4, 128))


def face_apply(finv, rows):
    turned = jnp.transpose(rows)
    outs = [jnp.sum(finv[m] * turned[:, m : m + 1], axis=0, keepdims=True) for m in range(7)]
    return jnp.concatenate(outs + [jnp.zeros((1, NF), F32)], axis=0)


def smem():
    return pl.BlockSpec(memory_space=pltpu.SMEM)


def vmem():
    return pl.BlockSpec(memory_space=pltpu.VMEM)


def faces(place, live, *packets):
    return pl.pallas_call(
        face_kernel,
        in_specs=[smem(), smem()] + [vmem()] * 9,
        out_shape=[
            jax.ShapeDtypeStruct((7, NF, NF), F32),
            jax.ShapeDtypeStruct((7, 48, NF), F32),
            jax.ShapeDtypeStruct((8, NF), F32),
            jax.ShapeDtypeStruct((8, NF), F32),
            jax.ShapeDtypeStruct((NCOR, 8), F32),
            jax.ShapeDtypeStruct((DEV, 4, 128), F32),
        ],
        scratch_shapes=[
            pltpu.VMEM((7, NF, NF), BF16),
            pltpu.VMEM((7, NF, NF), BF16),
            pltpu.VMEM((7, NF, NF), F32),
        ],
        compiler_params=pltpu.CompilerParams(vmem_limit_bytes=40 * 2**20),
        cost_estimate=pl.CostEstimate(flops=5 * 10**9, transcendentals=0, bytes_accessed=10 * 2**20),
        name="faces",
    )(place, live, *packets)


def owner_kernel(got, inverse, out, sums, grid):
    grid[...] = jnp.zeros((VC, 128), F32)
    total = jnp.zeros((1, 128), F32)
    for iy in range(GRID_Y):
        part = got[iy, 0:4, :]
        for ix in range(1, GRID_X):
            part = part + got[ix * GRID_Y + iy, 0:4, :]
        grid[iy : iy + 4, :] = grid[iy : iy + 4, :] + part
        total = total + part[0:1, :]
    sums[...] = jnp.broadcast_to(total, (8, 128))
    partial = jnp.zeros((16, 128), F32)
    for col in range(1, 18):
        partial = partial + inverse[col] * grid[col : col + 1, :]
    column = jnp.sum(partial, axis=1, keepdims=True)
    line = jnp.sum(jnp.where(iota((16, 128), 0) == iota((16, 128), 1), column, 0.0), axis=0, keepdims=True)
    out[...] = jnp.broadcast_to(line, (DEV, 128))


def owners(got, inverse):
    return pl.pallas_call(
        owner_kernel,
        out_shape=[jax.ShapeDtypeStruct((DEV, 128), F32), jax.ShapeDtypeStruct((8, 128), F32)],
        scratch_shapes=[pltpu.VMEM((VC, 128), F32)],
        cost_estimate=pl.CostEstimate(flops=10**6, transcendentals=0, bytes_accessed=2**20),
        name="owners",
    )(got, inverse)


def coarse_values(slots, coarse):
    lane = iota((NCOR, 128), 1).astype(F32)
    owner_rows = []
    places = []
    for g in range(8):
        number = slots[:, g : g + 1]
        owner = jnp.floor((number + 0.5) * (1.0 / OWN))
        places.append(number - OWN * owner)
        owner_rows.append(jnp.where(lane == owner, 1.0, 0.0))
    picked = lax.dot_general(
        jnp.concatenate(owner_rows, axis=0),
        coarse[...],
        (((1,), (0,)), ((), ())),
        precision=HIGHEST,
        preferred_element_type=F32,
    )
    return [
        jnp.sum(jnp.where(lane == places[g], picked[g * NCOR : (g + 1) * NCOR], 0.0), axis=1, keepdims=True)
        for g in range(8)
    ]


def prolong(tmap, values):
    outs = []
    for m in range(7):
        column = jnp.concatenate([values[GROUPS[m][0]], values[GROUPS[m][1]]], axis=0)
        outs.append(jnp.sum(tmap[m] * column, axis=0, keepdims=True))
    return jnp.concatenate(outs + [jnp.zeros((1, NF), F32)], axis=0)


def subdomain_apply(s_ref, vector):
    turned = jnp.transpose(vector)
    rows = []
    for s in range(2):
        across = [None] * 4
        upright = [None] * 4
        for f in range(4):
            column = turned[:, FACE[s][f] : FACE[s][f] + 1]
            for g in range(f, 4):
                block = s_ref[s, f * NF : (f + 1) * NF, g * NF : (g + 1) * NF]
                down = jnp.sum(block * column, axis=0, keepdims=True)
                across[g] = down if across[g] is None else across[g] + down
                if g > f:
                    m = FACE[s][g]
                    side = row_dot(block, vector[m : m + 1, :])
                    upright[f] = side if upright[f] is None else upright[f] + side
        columns = jnp.concatenate(
            [jnp.broadcast_to(upright[f], (NF, 128)) if f < 3 else jnp.zeros((NF, 128), F32) for f in range(4)], axis=1
        )
        lane_pick = jnp.concatenate([columns[:, f * 128 : f * 128 + 1] for f in range(4)] * 2, axis=1)
        flipped = jnp.transpose(lane_pick)
        for f in range(4):
            rows.append(across[f] + flipped[f : f + 1, :])
    return jnp.concatenate(rows, axis=0)


def restrict(place, tmap, image):
    gathered = {}

    def gather(g, value):
        gathered[g] = value if g not in gathered else gathered[g] + value

    for m in range(7):
        line = None
        for s in range(2):
            for f in range(4):
                if FACE[s][f] == m:
                    row = image[s * 4 + f : s * 4 + f + 1, :]
                    line = row if line is None else line + row
        gather(GROUPS[m][0], row_dot(tmap[m, 0:NCOR], line))
        gather(GROUPS[m][1], row_dot(tmap[m, NCOR:], line))
    return spread_window(place, gathered)


def post(place, live, image, send):
    me = place[0] * GRID_Y + place[1]

    def put(target, slot, row):
        send[target, slot : slot + 1, :] = image[row : row + 1, 0:128]
        send[target, slot + 1 : slot + 2, :] = image[row : row + 1, 128:256]

    @pl.when(live[0] > 0.0)
    def _():
        put(me - GRID_Y, 4, 0)

    @pl.when(live[1] > 0.0)
    def _():
        put(me + GRID_Y, 4, 5)

    @pl.when(live[2] > 0.0)
    def _():
        put(me - 1, 4, 2)
        put(me - 1, 6, 6)

    @pl.when(live[3] > 0.0)
    def _():
        put(me + 1, 4, 3)
        put(me + 1, 6, 7)


def meet(place, live, image, got):
    me = place[0] * GRID_Y + place[1]

    def read(source, slot, alive):
        at = jnp.clip(source, 0, DEV - 1)
        row = jnp.concatenate([got[at, slot : slot + 1, :], got[at, slot + 1 : slot + 2, :]], axis=1)
        return jnp.where(alive > 0.0, row, 0.0)

    def mine(row):
        return image[row : row + 1, :]

    return jnp.concatenate(
        [
            live[0] * (mine(0) + read(me - GRID_Y, 4, live[0])),
            mine(1) + mine(4),
            live[1] * (mine(5) + read(me + GRID_Y, 4, live[1])),
            live[2] * (mine(2) + read(me - 1, 4, live[2])),
            live[2] * (mine(6) + read(me - 1, 6, live[2])),
            live[3] * (mine(3) + read(me + 1, 4, live[3])),
            live[3] * (mine(7) + read(me + 1, 6, live[3])),
            jnp.zeros((1, NF), F32),
        ],
        axis=0,
    )


def shared_dot(first, second):
    weight = jnp.where(iota((8, NF), 0) == 1, 1.0, 0.5)
    return jnp.sum(weight * first * second)


def sides(vector):
    return jnp.concatenate([vector[m : m + 1, :] for s in range(2) for m in FACE[s]], axis=0)


def tag(row, *scalars):
    lane = iota((1, 128), 1)
    for at, value in scalars:
        row = jnp.where(lane == at, value, row)
    return row


def first_kernel(place, live, s_ref, tmap, resid, smooth, slots, coarse, z_out, c_out, send):
    z = smooth[...] + prolong(tmap, coarse_values(slots, coarse))
    z_out[...] = z
    image = subdomain_apply(s_ref, z)
    c_out[...] = image
    cols = restrict(place, tmap, image)
    gamma = shared_dot(resid[...], z)
    delta = jnp.sum(sides(z) * image)
    cols[0] = tag(cols[0], (120, gamma), (121, delta))
    window = jnp.concatenate(cols + [jnp.zeros((4, 128), F32)], axis=0)
    send[...] = jnp.broadcast_to(window[None], (DEV, 8, 128))
    post(place, live, image, send)


def first(place, live, *rest):
    return pl.pallas_call(
        first_kernel,
        in_specs=[smem(), smem()] + [vmem()] * 6,
        out_shape=[
            jax.ShapeDtypeStruct((8, NF), F32),
            jax.ShapeDtypeStruct((8, NF), F32),
            jax.ShapeDtypeStruct((DEV, 8, 128), F32),
        ],
        compiler_params=pltpu.CompilerParams(vmem_limit_bytes=40 * 2**20),
        cost_estimate=pl.CostEstimate(flops=10**7, transcendentals=0, bytes_accessed=10 * 2**20),
        name="first",
    )(place, live, *rest)


def pick_lane(row, at):
    return jnp.sum(jnp.where(iota((1, 128), 1) == at, row, 0.0))


def second_kernel(place, live, s_ref, finv, tmap, resid, z_old, c_old, slots, coarse, sums, got, z_out, c_out, w_out, r_out, send):
    gamma = pick_lane(sums[0:1, :], 120)
    delta = pick_lane(sums[0:1, :], 121)
    alpha = gamma / delta
    w = meet(place, live, c_old, got)
    w_out[...] = w
    y = face_apply(finv, w) + prolong(tmap, coarse_values(slots, coarse))
    z = z_old[...] - alpha * y
    r = resid[...] - alpha * w
    z_out[...] = z
    r_out[...] = r
    image = subdomain_apply(s_ref, z)
    c_out[...] = image
    gamma_new = shared_dot(r, z)
    new_new = jnp.sum(sides(z) * image)
    old_new = jnp.sum(sides(z_old[...]) * image)
    new_old = jnp.sum(sides(z) * c_old[...])
    line = tag(
        jnp.zeros((1, 128), F32), (0, gamma_new), (1, new_new), (2, old_new), (3, new_old)
    )
    window = jnp.concatenate([line, jnp.zeros((7, 128), F32)], axis=0)
    send[...] = jnp.broadcast_to(window[None], (DEV, 8, 128))
    post(place, live, image, send)


def second(place, live, *rest):
    small = jax.ShapeDtypeStruct((8, NF), F32)
    return pl.pallas_call(
        second_kernel,
        in_specs=[smem(), smem()] + [vmem()] * 10,
        out_shape=[small, small, small, small, jax.ShapeDtypeStruct((DEV, 8, 128), F32)],
        compiler_params=pltpu.CompilerParams(vmem_limit_bytes=40 * 2**20),
        cost_estimate=pl.CostEstimate(flops=10**7, transcendentals=0, bytes_accessed=12 * 2**20),
        name="second",
    )(place, live, *rest)


def last_kernel(place, live, z_old, w_old, z_new, c_new, resid, sums, got, x_out, r_out):
    line = got[0, 0:1, :]
    for e in range(1, DEV):
        line = line + got[e, 0:1, :]
    gamma = pick_lane(sums[0:1, :], 120)
    delta = pick_lane(sums[0:1, :], 121)
    alpha = gamma / delta
    gamma_new = pick_lane(line, 0)
    beta = gamma_new / gamma
    curve = pick_lane(line, 1) + beta * (pick_lane(line, 2) + pick_lane(line, 3)) + beta * beta * delta
    alpha_new = gamma_new / curve
    w = meet(place, live, c_new[...], got)
    search = z_new[...] + beta * z_old[...]
    along = w + beta * w_old[...]
    x = sides(alpha * z_old[...] + alpha_new * search)
    r = sides(resid[...] - alpha_new * along)
    for s in range(2):
        x_out[s, 0] = x[4 * s : 4 * s + 4]
        r_out[s, 0] = r[4 * s : 4 * s + 4]


def last(place, live, *rest):
    out = jax.ShapeDtypeStruct((2, 1, 4, NF), F32)
    return pl.pallas_call(
        last_kernel,
        in_specs=[smem(), smem()] + [vmem()] * 7,
        out_shape=[out, out],
        cost_estimate=pl.CostEstimate(flops=10**6, transcendentals=0, bytes_accessed=2**20),
        name="last",
    )(place, live, *rest)


def shift(value, axis, steps):
    count = lax.axis_size(axis)
    first_, last_ = max(0, -steps), min(count, count - steps)
    return lax.ppermute(value, axis, [(source, source + steps) for source in range(first_, last_)])


def exchange(packet):
    return lax.all_to_all(packet, GX_GY, 0, 0, tiled=True)


def vertex_table(corners, ix, iy):
    number = corners.astype(F32) + 1.0
    upper = number[:, :12].reshape(2, 2, 6)
    lower = number[1:, 12:].reshape(1, 2, 6)
    rows = jnp.concatenate([upper, lower], axis=0)
    keep = jnp.stack([jnp.bool_(True), jnp.bool_(True), ix == GRID_X - 1])
    rows = jnp.where(keep[:, None, None], rows, 0.0)
    line = jnp.transpose(rows, (1, 0, 2)).reshape(2, 18)
    line = jnp.where(jnp.stack([jnp.bool_(True), iy == GRID_Y - 1])[:, None], line, 0.0)
    return lax.dynamic_update_slice(jnp.zeros((2, 128), F32), line, (0, 12 * ix))


def shards(inverse, couple, stiff, basis, loads, order, corner_index, coarse_inverse):
    ix = lax.axis_index(GX)
    iy = lax.axis_index(GY)
    corners = corner_index.reshape(2, NCOR)
    place = jnp.stack([ix, iy]).astype(jnp.int32)
    live = jnp.stack([ix > 0, ix < GRID_X - 1, iy > 0, iy < GRID_Y - 1]).astype(F32)
    table = exchange(jnp.broadcast_to(vertex_table(corners, ix, iy)[None], (DEV, 2, 128)))
    index = jnp.pad(corners.astype(F32), ((0, 0), (0, NF - NCOR))).reshape(2, 1, NF)
    s_full, p_in, p_n, p_s, p_w, p_e = schur(order, inverse, couple, stiff, basis, loads, index)
    q_s = shift(p_n, GX, -1)
    q_n = shift(p_s, GX, 1)
    q_e = shift(p_w, GY, -1)
    q_w = shift(p_e, GY, 1)
    columns = jnp.pad(jnp.transpose(coarse_inverse), ((0, 2), (0, 0)))
    coarse = vertex_order(table, columns)
    finv, tmap, resid, smooth, slots, send = faces(place, live, p_in, p_n, p_s, p_w, p_e, q_n, q_s, q_w, q_e)
    values, _ = owners(exchange(send), coarse)
    z0, c0, send = first(place, live, s_full, tmap, resid, smooth, slots, exchange(values))
    got = exchange(send)
    values, sums = owners(got, coarse)
    z1, c1, w0, r1, send = second(
        place, live, s_full, finv, tmap, resid, z0, c0, slots, exchange(values), sums, got
    )
    got = exchange(send)
    return tuple(last(place, live, z0, w0, z1, c1, r1, sums, got))


def solution(mesh):
    torus = Mesh(mesh.devices.reshape(4, 2, 4, 2, 2), GX_GY)
    in_specs = (
        P(GX, GY, None, None),
        P(GX, GY, None, None),
        P(GX, GY, None, None, None),
        P(GX, GY, None, None),
        P(GX, GY, None, None),
        P(GX, GY, None, None),
        P(GX, GY, None),
        P(None, GX_GY),
    )
    out_specs = (P(GX, GY, None, None), P(GX, GY, None, None))
    return jax.shard_map(shards, mesh=torus, in_specs=in_specs, out_specs=out_specs, check_vma=False)
```

time: 958 us -> 189 us (0.20); the launches traced: 947 us -> 188 us
  other arithmetic: 246 us -> 1.07 us
  local copies, waits for them, and re-layouts: 239 us -> 21.1 us
  blocking collectives: 278 us -> 64.4 us
  matrix products: 88.5 us -> 0 us
  Pallas kernels: 0 us -> 51.5 us
  starting transfers between devices: 70.9 us -> 40.6 us
  between operations: 10.7 us -> 0.84 us
    another operation x20 -> x2, other arithmetic: 230 us -> 0.15 us  [the longest x1 0.08 us: vertex_table(): jnp.stack([jnp.bool_(True), iy == GRID_Y - 1])[:, None]]
    gather x19 -> x0, local copies, waits for them, and re-layouts: 185 us -> none  [reorder(): return jnp.take_along_axis(values, positions, axis=-1)]
    psum x20 -> x0, blocking collectives: 143 us -> none  [by_axis(): array = lax.psum(array, axis)]
    unnamed x2 -> x0, blocking collectives: 135 us -> none
    dot_general x32 -> x0, matrix products: 72.8 us -> none  [the longest x1 16.5 us: shards(): jnp.einsum('sij,sjk->sik', inverse_mat, couple, preferred_element_type=jn...]
    all_to_all x0 -> x4, blocking collectives: none -> 64.4 us  [exchange(): return lax.all_to_all(packet, GX_GY, 0, 0, tiled=True)]
    ppermute x24 -> x4, starting transfers between devices: 70.9 us -> 12 us  [shift(): lax.ppermute(value, axis, [(source, source + steps) for source in range(f...]
    pallas_call x0 -> x8, Pallas kernels: none -> 51.6 us  [the longest x1 26 us: schur(): pl.pallas_call(schur_kernel, grid=(2, STEPS), in_specs=[pl.BlockSpec((Non...]
  transfers between devices with their start and end apart: 24 -> 6, of which waited for: 7 -> 1; matrix products, arithmetic and copies ran while one was open for 34% -> 1% of each run, Pallas kernels for 0% -> 7%
where the time goes in v1:
time: 189 us; the launch traced here: 188 us
  blocking collectives  64.4 us (34%)
  Pallas kernels  51.5 us (27%)
  starting transfers between devices  40.6 us (21%)
  local copies, waits for them, and re-layouts  21.1 us (11%)
  waiting for transfers between devices  8.41 us (4%)
    all_to_all x4, blocking collectives, exchange(): return lax.all_to_all(packet, GX_GY, 0, 0, tiled=True)  64.4 us
    all_to_all x2, starting transfers between devices, exchange(): return lax.all_to_all(packet, GX_GY, 0, 0, tiled=True)  28.6 us
    pallas_call x1, Pallas kernels, schur(): pl.pallas_call(schur_kernel, grid=(2, STEPS), in_specs=[pl.BlockSpec((Non...  26 us
    unnamed x44, local copies, waits for them, and re-layouts  18.4 us
    pallas_call x1, Pallas kernels, faces(): pl.pallas_call(face_kernel, in_specs=[smem(), smem()] + [vmem()] * 9, out...  12.1 us
    ppermute x4, starting transfers between devices, shift(): lax.ppermute(value, axis, [(source, source + steps) for source in range(f...  12 us
    all_to_all x2, waiting for transfers between devices, exchange(): return lax.all_to_all(packet, GX_GY, 0, 0, tiled=True)  8.4 us
  transfers between devices with their start and end apart: 6, of which 1 were waited for; matrix products, arithmetic and copies ran while one was open for 1% of the time, Pallas kernels for 7%

profile of v1, /device:TPU:1, one launch (start us, length us, event | category | flops | bytes accessed | tf_op | source)
XLA Modules:
  0.0 187.9 jit_solution(2532635611426737502)
XLA Ops:
  0.6 0.7 convert_element_type.15
  1.3 0.6 reshape.43.index
  1.9 26.0 %schur.1 = (f32[2,1024,1024]{2,1,0:T(8,128)}, f32[2,288,256]{2,1,0:T(8,128)}, f32[288,256]{1,0:T(8,128)}, f32[288,256]{1,0:T(8,128)}, f32[2,288,256]{2,1,0:T(8,128)}, /*index=5*/f32[2,288,256]{2,1,0:T(8,128)}) custom-call(s32[2,1,4,256]{3,2,1,0:T(4,128)} %order.1, bf16[2,1,1536,1536]{3,2,1,0:T(8,128)(2,1)} %inverse.1, bf16[2,1,1536,1024]{3,2,1,0:T(8,128)(2,1)} %couple.1, ...), custom_call_target="tpu_custom_call" | custom-call | flops 16000000000 | bytes 33554432 | tf_op jit(solution)/shard_map/schur/pallas_call | solution.py:113
  27.9 5.6 %collective-permute-start = (f32[288,256]{1,0:T(8,128)}, f32[288,256]{1,0:T(8,128)S(1)}, u32[]{:S(2)}, u32[]{:S(2)}) collective-permute-start(f32[288,256]{1,0:T(8,128)} %get-tuple-element.28.p_s), channel_id=1, source_target_pairs={{0,16},{16,32},{32,48},{48,64},{64,80},{80,96},{96,112},{1,17},{17... | collective-permute-start | bytes 884744 | tf_op jit(solution)/shard_map/ppermute | solution.py:617
  33.6 1.3 collective-permute-start.1
  34.9 3.1 %collective-permute-start.2 = (f32[2,288,256]{2,1,0:T(8,128)}, f32[2,288,256]{2,1,0:T(8,128)S(1)}, u32[]{:S(2)}, u32[]{:S(2)}) collective-permute-start(f32[2,288,256]{2,1,0:T(8,128)} %get-tuple-element.30.p_e), channel_id=1, source_target_pairs={{0,1},{1,2},{2,3},{3,4},{4,5},{5,6},{6,7},{7,8},{8,9},{9,10},{10,1... | collective-permute-start | bytes 1769480 | tf_op jit(solution)/shard_map/ppermute | solution.py:617
  38.0 1.9 %collective-permute-start.3 = (f32[2,288,256]{2,1,0:T(8,128)}, f32[2,288,256]{2,1,0:T(8,128)S(1)}, u32[]{:S(2)}, u32[]{:S(2)}) collective-permute-start(f32[2,288,256]{2,1,0:T(8,128)} %get-tuple-element.29.p_w), channel_id=1, source_target_pairs={{1,0},{2,1},{3,2},{4,3},{5,4},{6,5},{7,6},{8,7},{9,8},{10,9},{11,1... | collective-permute-start | bytes 1769480 | tf_op jit(solution)/shard_map/ppermute | solution.py:617
  40.0 0.1 slice_reduce_fusion
  40.1 0.1 reshape.45
  40.1 0.1 reshape.44
  40.2 0.1 stack.47
  40.3 0.1 fusion
  40.4 0.1 reshape.46
  40.5 0.1 pad_add_fusion
  40.5 0.1 broadcast_select_fusion
  40.6 0.1 dynamic_update_slice.5
  40.7 0.7 broadcast_in_dim.40
  41.4 13.4 %all-to-all-start.1 = ((f32[128,2,128]{2,1,0:T(2,128)}), f32[128,2,128]{2,1,0:T(2,128)S(1)}, u32[]{:S(2)}, u32[]{:S(2)}) async-start(f32[128,2,128]{2,1,0:T(2,128)} %broadcast_in_dim.40), calls=%async_computation.1 | async-start | bytes 262144 | tf_op jit(solution)/shard_map/all_to_all | solution.py:621
  54.8 0.1 pad_add_fusion.1.place
  54.9 0.1 add_convert_fusion.live
  55.0 0.0 collective-permute-done.q_n
  55.0 0.7 copy-done.16
  55.7 0.0 collective-permute-done.1.q_s
  55.7 0.7 copy-done.18
  56.4 0.0 collective-permute-done.2.q_w
  56.4 0.0 collective-permute-done.3.q_e
  56.4 1.1 copy-done.12
  57.5 1.1 copy-done.13
  58.5 1.0 copy-done.14
  59.5 1.0 copy-done.15
  60.5 1.0 copy-done.17
  61.4 1.0 copy-done.19
  62.4 1.1 copy-done.20
  63.4 12.1 %faces.1 = (f32[7,256,256]{2,1,0:T(8,128)S(1)}, f32[7,48,256]{2,1,0:T(8,128)S(1)}, f32[8,256]{1,0:T(8,128)S(1)}, f32[8,256]{1,0:T(8,128)S(1)}, f32[24,8]{1,0:T(8,128)S(1)}, /*index=5*/f32[128,4,128]{2,1,0:T(4,128)}) custom-call(s32[2]{0:T(128)S(1)} %pad_add_fusion.1.place, f32[4]{0:T(128)S(1)} %add_convert_fusion.live, f32[2,288,256]{2,1,0:T(8,128)S(1)} %copy-done.20, ...), custom_call_target="tpu_custom_call" | custom-call | flops 5000000000 | bytes 10485760 | tf_op jit(solution)/shard_map/faces/pallas_call | solution.py:320
  75.5 0.0 all-to-all-done.1.table
  75.5 15.1 %all-to-all-start = ((f32[128,4,128]{2,1,0:T(4,128)}), f32[128,4,128]{2,1,0:T(4,128)S(1)}, u32[]{:S(2)}, u32[]{:S(2)}) async-start(f32[128,4,128]{2,1,0:T(4,128)} %get-tuple-element.35), calls=%async_computation | async-start | bytes 524288 | tf_op jit(solution)/shard_map/all_to_all | solution.py:621
  90.7 0.9 pad.10.columns
  91.6 1.4 vertex_order.1.inverse
  93.0 0.7 copy-done.3
  93.7 8.4 %all-to-all-done.got = f32[128,4,128]{2,1,0:T(4,128)S(1)} async-done(((f32[128,4,128]{2,1,0:T(4,128)}), f32[128,4,128]{2,1,0:T(4,128)S(1)}, u32[]{:S(2)}, u32[]{:S(2)}) %all-to-all-start) | async-done | bytes 262176 | tf_op jit(solution)/shard_map/all_to_all | solution.py:621
  102.1 0.7 copy-done.21
  102.8 1.8 owners.2
  104.6 14.0 %all_to_all.42 = f32[128,1,128]{2,1,0:T(1,128)S(1)} all-to-all(f32[128,1,128]{2,1,0:T(1,128)} %bitcast.24), channel_id=1, replica_groups=mesh['gx_0'=4,'gx_1'=2,'gy_0'=4,'gy_1'=2,'gy_2'=2] {'gx_0','gx_1','gy_0'..., dimensions={0} | all-to-all | bytes 131072 | tf_op jit(solution)/shard_map/all_to_all | solution.py:621
  118.7 3.4 %copy-done = f32[2,1024,1024]{2,1,0:T(8,128)S(1)} copy-done((f32[2,1024,1024]{2,1,0:T(8,128)S(1)}, f32[2,1024,1024]{2,1,0:T(8,128)}, u32[]{:S(2)}) %copy-start) | copy-done | bytes 8388632
  122.1 2.7 %first.1 = (f32[8,256]{1,0:T(8,128)S(1)}, f32[8,256]{1,0:T(8,128)S(1)}, f32[128,8,128]{2,1,0:T(8,128)S(1)}) custom-call(s32[2]{0:T(128)S(1)} %pad_add_fusion.1.place, f32[4]{0:T(128)S(1)} %add_convert_fusion.live, f32[2,1024,1024]{2,1,0:T(8,128)S(1)} %copy-done, f32[7,48,256]{2,1,0:T(8,128)S(1)} %get-tuple-element.31.tmap, ...), custom_call_target="tpu_custom_call" | custom-call | flops 10000000 | bytes 10485760 | tf_op jit(solution)/shard_map/first/pallas_call | solution.py:527
  124.7 0.0 copy-start.4
  124.7 18.2 %all_to_all.43.got = f32[128,8,128]{2,1,0:T(8,128)} all-to-all(f32[128,8,128]{2,1,0:T(8,128)S(1)} %get-tuple-element.40), channel_id=1, replica_groups=mesh['gx_0'=4,'gx_1'=2,'gy_0'=4,'gy_1'=2,'gy_2'=2] {'gx_0','gx_1','gy_0'..., dimensions={0} | all-to-all | bytes 1048576 | tf_op jit(solution)/shard_map/all_to_all | solution.py:621
  142.9 1.9 %owners.3 = (f32[128,128]{1,0:T(8,128)}, f32[8,128]{1,0:T(8,128)}) custom-call(f32[128,8,128]{2,1,0:T(8,128)} %all_to_all.43.got, f32[24,16,128]{2,1,0:T(8,128)} %copy-done.3), custom_call_target="tpu_custom_call" | custom-call | flops 1000000 | bytes 1048576 | tf_op jit(solution)/shard_map/owners/pallas_call | solution.py:361
  144.8 14.0 %all_to_all.44 = f32[128,1,128]{2,1,0:T(1,128)S(1)} all-to-all(f32[128,1,128]{2,1,0:T(1,128)} %bitcast.25), channel_id=1, replica_groups=mesh['gx_0'=4,'gx_1'=2,'gy_0'=4,'gy_1'=2,'gy_2'=2] {'gx_0','gx_1','gy_0'..., dimensions={0} | all-to-all | bytes 131072 | tf_op jit(solution)/shard_map/all_to_all | solution.py:621
  158.8 0.0 copy-done.11
  158.8 0.0 copy-done.10
  158.8 3.4 %copy-done.1 = f32[2,1024,1024]{2,1,0:T(8,128)S(1)} copy-done((f32[2,1024,1024]{2,1,0:T(8,128)S(1)}, f32[2,1024,1024]{2,1,0:T(8,128)}, u32[]{:S(2)}) %copy-start.1) | copy-done | bytes 8388632
  162.2 1.0 copy-done.2
  163.2 0.7 copy-done.5
  163.9 3.6 %second.1 = (f32[8,256]{1,0:T(8,128)S(1)}, f32[8,256]{1,0:T(8,128)S(1)}, f32[8,256]{1,0:T(8,128)S(1)}, f32[8,256]{1,0:T(8,128)S(1)}, f32[128,8,128]{2,1,0:T(8,128)S(1)}) custom-call(s32[2]{0:T(128)S(1)} %pad_add_fusion.1.place, f32[4]{0:T(128)S(1)} %add_convert_fusion.live, f32[2,1024,1024]{2,1,0:T(8,128)S(1)} %copy-done.1, ...), custom_call_target="tpu_custom_call" | custom-call | flops 10000000 | bytes 12582912 | tf_op jit(solution)/shard_map/second/pallas_call | solution.py:572
  167.5 0.0 copy-start.6
  167.5 0.0 copy-start.7
  167.6 0.0 copy-start.8
  167.6 0.0 copy-start.9
  167.6 18.2 %all_to_all.45.got = f32[128,8,128]{2,1,0:T(8,128)} all-to-all(f32[128,8,128]{2,1,0:T(8,128)S(1)} %get-tuple-element.47), channel_id=1, replica_groups=mesh['gx_0'=4,'gx_1'=2,'gy_0'=4,'gy_1'=2,'gy_2'=2] {'gx_0','gx_1','gy_0'..., dimensions={0} | all-to-all | bytes 1048576 | tf_op jit(solution)/shard_map/all_to_all | solution.py:621
  185.8 0.0 copy-done.6
  185.8 0.0 copy-done.7
  185.8 0.0 copy-done.8
  185.8 2.1 %last.1 = (f32[2,1,4,256]{3,2,1,0:T(4,128)}, f32[2,1,4,256]{3,2,1,0:T(4,128)}) custom-call(s32[2]{0:T(128)} %copy-done.11, f32[4]{0:T(128)} %copy-done.10, f32[8,256]{1,0:T(8,128)} %copy-done.4, f32[8,256]{1,0:T(8,128)} %copy-done.8, f32[8,256]{1,0:T(8,128)} %copy-done.6, f32[8,256]{1,0:T(8,128)} %copy-done.7, f32[8,256]{1,0:T(8,128)} %copy-done.9, ...), custom_call_target="tpu_custom_call" | custom-call | flops 1000000 | bytes 1048576 | tf_op jit(solution)/shard_map/last/pallas_call | solution.py:605
  (23 shorter events, 0.0 us)
Async XLA Ops:
  27.9 27.1 %collective-permute-start = (f32[288,256]{1,0:T(8,128)}, f32[288,256]{1,0:T(8,128)S(1)}, u32[]{:S(2)}, u32[]{:S(2)}) collective-permute-start(f32[288,256]{1,0:T(8,128)} %get-tuple-element.28.p_s), channel_id=1, source_target_pairs={{0,16},{16,32},{32,48},{48,64},{64,80},{80,96},{96,112},{1,17},{17... | collective-permute-start | bytes 884744 | tf_op jit(solution)/shard_map/ppermute | solution.py:617
  33.6 22.1 %collective-permute-start.1 = (f32[288,256]{1,0:T(8,128)}, f32[288,256]{1,0:T(8,128)S(1)}, u32[]{:S(2)}, u32[]{:S(2)}) collective-permute-start(f32[288,256]{1,0:T(8,128)} %get-tuple-element.27.p_n), channel_id=1, source_target_pairs={{16,0},{32,16},{48,32},{64,48},{80,64},{96,80},{112,96},{17,1},{33... | collective-permute-start | bytes 884744 | tf_op jit(solution)/shard_map/ppermute | solution.py:617
  34.9 21.5 %collective-permute-start.2 = (f32[2,288,256]{2,1,0:T(8,128)}, f32[2,288,256]{2,1,0:T(8,128)S(1)}, u32[]{:S(2)}, u32[]{:S(2)}) collective-permute-start(f32[2,288,256]{2,1,0:T(8,128)} %get-tuple-element.30.p_e), channel_id=1, source_target_pairs={{0,1},{1,2},{2,3},{3,4},{4,5},{5,6},{6,7},{7,8},{8,9},{9,10},{10,1... | collective-permute-start | bytes 1769480 | tf_op jit(solution)/shard_map/ppermute | solution.py:617
  38.0 18.4 %collective-permute-start.3 = (f32[2,288,256]{2,1,0:T(8,128)}, f32[2,288,256]{2,1,0:T(8,128)S(1)}, u32[]{:S(2)}, u32[]{:S(2)}) collective-permute-start(f32[2,288,256]{2,1,0:T(8,128)} %get-tuple-element.29.p_w), channel_id=1, source_target_pairs={{1,0},{2,1},{3,2},{4,3},{5,4},{6,5},{7,6},{8,7},{9,8},{10,9},{11,1... | collective-permute-start | bytes 1769480 | tf_op jit(solution)/shard_map/ppermute | solution.py:617
  41.4 34.2 %all-to-all-start.1 = ((f32[128,2,128]{2,1,0:T(2,128)}), f32[128,2,128]{2,1,0:T(2,128)S(1)}, u32[]{:S(2)}, u32[]{:S(2)}) async-start(f32[128,2,128]{2,1,0:T(2,128)} %broadcast_in_dim.40), calls=%async_computation.1 | async-start | bytes 262144 | tf_op jit(solution)/shard_map/all_to_all | solution.py:621
  54.9 103.9 %copy-start.11 = (s32[2]{0:T(128)}, s32[2]{0:T(128)S(1)}, u32[]{:S(2)}) copy-start(s32[2]{0:T(128)S(1)} %pad_add_fusion.1.place) | copy-start | bytes 28
  55.0 103.8 %copy-start.10 = (f32[4]{0:T(128)}, f32[4]{0:T(128)S(1)}, u32[]{:S(2)}) copy-start(f32[4]{0:T(128)S(1)} %add_convert_fusion.live) | copy-start | bytes 52
  55.0 0.7 copy-start.16
  55.7 0.7 copy-start.18
  56.4 1.1 copy-start.12
  57.5 1.1 copy-start.13
  58.5 1.0 copy-start.14
  59.5 1.0 copy-start.15
  60.5 1.0 copy-start.17
  61.4 1.0 copy-start.19
  62.4 1.1 copy-start.20
  75.5 26.6 %all-to-all-start = ((f32[128,4,128]{2,1,0:T(4,128)}), f32[128,4,128]{2,1,0:T(4,128)S(1)}, u32[]{:S(2)}, u32[]{:S(2)}) async-start(f32[128,4,128]{2,1,0:T(4,128)} %get-tuple-element.35), calls=%async_computation | async-start | bytes 524288 | tf_op jit(solution)/shard_map/all_to_all | solution.py:621
  93.0 0.7 copy-start.3
  102.1 0.7 copy-start.21
  118.7 3.4 %copy-start = (f32[2,1024,1024]{2,1,0:T(8,128)S(1)}, f32[2,1024,1024]{2,1,0:T(8,128)}, u32[]{:S(2)}) copy-start(f32[2,1024,1024]{2,1,0:T(8,128)} %get-tuple-element.25.s_ref) | copy-start | bytes 25165828
  124.7 61.1 %copy-start.4 = (f32[8,256]{1,0:T(8,128)}, f32[8,256]{1,0:T(8,128)S(1)}, u32[]{:S(2)}) copy-start(f32[8,256]{1,0:T(8,128)S(1)} %get-tuple-element.37.z_old) | copy-start | bytes 24580
  158.8 3.4 %copy-start.1 = (f32[2,1024,1024]{2,1,0:T(8,128)S(1)}, f32[2,1024,1024]{2,1,0:T(8,128)}, u32[]{:S(2)}) copy-start(f32[2,1024,1024]{2,1,0:T(8,128)} %get-tuple-element.25.s_ref) | copy-start | bytes 25165828
  162.2 1.0 copy-start.2
  163.2 0.7 copy-start.5
  167.5 18.2 %copy-start.6 = (f32[8,256]{1,0:T(8,128)}, f32[8,256]{1,0:T(8,128)S(1)}, u32[]{:S(2)}) copy-start(f32[8,256]{1,0:T(8,128)S(1)} %get-tuple-element.44.z_new) | copy-start | bytes 24580
  167.5 18.2 %copy-start.7 = (f32[8,256]{1,0:T(8,128)}, f32[8,256]{1,0:T(8,128)S(1)}, u32[]{:S(2)}) copy-start(f32[8,256]{1,0:T(8,128)S(1)} %get-tuple-element.45.c_new) | copy-start | bytes 24580
  167.6 18.2 %copy-start.8 = (f32[8,256]{1,0:T(8,128)}, f32[8,256]{1,0:T(8,128)S(1)}, u32[]{:S(2)}) copy-start(f32[8,256]{1,0:T(8,128)S(1)} %get-tuple-element.43.w_old) | copy-start | bytes 24580
  167.6 18.2 %copy-start.9 = (f32[8,256]{1,0:T(8,128)}, f32[8,256]{1,0:T(8,128)S(1)}, u32[]{:S(2)}) copy-start(f32[8,256]{1,0:T(8,128)S(1)} %get-tuple-element.46.resid) | copy-start | bytes 24580

commit v2 on v1

v2 whole, which is shorter than its diff:
```python
import jax
import jax.numpy as jnp
from jax import lax
from jax.experimental import pallas as pl
from jax.experimental.pallas import tpu as pltpu
from jax.sharding import Mesh
from jax.sharding import PartitionSpec as P

GX = ("gx_0", "gx_1")
GY = ("gy_0", "gy_1", "gy_2")
GX_GY = GX + GY

NI = 1536
NF = 256
NCOR = 24
NCOARSE = 1792
OWN = 14
GRID_X = 8
GRID_Y = 16
DEV = 128
PKT = 288
ONE = 160
TWO = 312
HALF = NF // 2
STEPS = 3
CHUNK = NI // STEPS
VC = 24
F32 = jnp.float32
BF16 = jnp.bfloat16
HIGHEST = lax.Precision.HIGHEST

FACE = ((0, 1, 3, 5), (1, 2, 4, 6))
GROUPS = ((0, 2), (0, 1), (1, 3), (0, 4), (1, 5), (0, 6), (1, 7))
GROUP_ROW = (0, 1, -1, 2, 0, 1, 0, 1)
GROUP_COL = (1, 1, 1, 1, 0, 0, 2, 2)


def nn(a, b):
    return lax.dot_general(a, b, (((1,), (0,)), ((), ())), preferred_element_type=F32)


def nt(a, b):
    return lax.dot_general(a, b, (((1,), (1,)), ((), ())), preferred_element_type=F32)


def split2(x):
    hi = x.astype(BF16)
    return hi, (x - hi.astype(F32)).astype(BF16)


def split3(x):
    hi = x.astype(BF16)
    rest = x - hi.astype(F32)
    mid = rest.astype(BF16)
    return hi, mid, (rest - mid.astype(F32)).astype(BF16)


def iota(shape, dim):
    return lax.broadcasted_iota(jnp.int32, shape, dim)


BLOCK = {}
for f_ in range(4):
    for g_ in range(f_, 4):
        BLOCK[f_, g_] = len(BLOCK)


def schur_kernel(order, inverse, couple, stiff, basis, loads, index, s_out, p_in, p_n, p_s, p_w, p_e, t_n, t_s, t_w, t_e, ct, prod, pick):
    sub = pl.program_id(0)
    step = pl.program_id(1)

    @pl.when(step == 0)
    def _():
        for f in range(4):
            chosen = (iota((NF, NF), 0) == order[f : f + 1, :]).astype(BF16)
            pick[f] = chosen
            ct[f * NF : (f + 1) * NF, :] = nt(chosen, couple[:, f * NF : (f + 1) * NF]).astype(BF16)

    prod[pl.ds(step * CHUNK, CHUNK), :] = nt(inverse[...], ct[...]).astype(BF16)

    @pl.when(step == STEPS - 1)
    def _():
        for f in range(4):
            rows = slice(f * NF, (f + 1) * NF)
            back = nn(ct[rows, :], prod[:, f * NF :])
            chosen = pick[f]
            canon = nt(nn(chosen, stiff[f]).astype(BF16), chosen)
            diag = canon - back[:, :NF]
            s_out[BLOCK[f, f]] = diag.astype(BF16)
            for g in range(f + 1, 4):
                s_out[BLOCK[f, g]] = (-back[:, (g - f) * NF : (g - f + 1) * NF]).astype(BF16)
            lowered = nt(basis[:, f * NF : (f + 1) * NF], chosen).astype(BF16)
            hi, lo = split2(diag)
            corner = nn(lowered, hi) + nn(lowered, lo)
            parts = jnp.concatenate(
                [part.astype(F32) for part in split3(jnp.broadcast_to(loads[f : f + 1, :], (8, NF)))], axis=0
            ).astype(BF16)
            placed = nt(parts, chosen)
            load = placed[0:8] + placed[8:16] + placed[16:24]

            def put(out, lead):
                out[lead + (slice(0, NF), slice(None))] = diag
                out[lead + (slice(NF, NF + NCOR), slice(None))] = corner
                out[lead + (slice(NF + NCOR, NF + NCOR + 8), slice(None))] = jnp.where(iota((8, NF), 0) == 0, load, 0.0)
                out[lead + (slice(NF + NCOR + 1, NF + NCOR + 2), slice(0, NCOR))] = index[...].astype(F32)

            def put_one(out):
                row, col = iota((HALF, HALF), 0), iota((HALF, HALF), 1)
                first_ = diag[:HALF, :HALF]
                out[0:HALF, 0:HALF] = jnp.where(row > col, first_, diag[HALF:, HALF:])
                out[0:HALF, HALF:] = diag[HALF:, :HALF]
                out[HALF : HALF + NCOR, :] = corner
                at = HALF + NCOR
                out[at : at + 8, :] = jnp.where(iota((8, NF), 0) == 0, load, 0.0)
                out[at + 1 : at + 2, 0:NCOR] = index[...].astype(F32)
                out[at + 2 : at + 3, 0:HALF] = jnp.sum(jnp.where(row == col, first_, 0.0), axis=0, keepdims=True)

            def put_two(out, kept):
                row, col = iota((NF, NF), 0), iota((NF, NF), 1)
                first_ = kept[0, 0:NF, :]
                out[0:NF, :] = jnp.where(row > col, first_, diag)
                out[NF : NF + NCOR, :] = kept[0, NF : NF + NCOR, :]
                out[NF + NCOR : NF + 2 * NCOR, :] = corner
                at = NF + 2 * NCOR
                out[at : at + 8, :] = jnp.where(iota((8, NF), 0) == 2, load, 0.0)
                out[at : at + 2, :] = kept[0, NF + NCOR : NF + NCOR + 2, :]
                out[at + 3 : at + 4, 0:NCOR] = index[...].astype(F32)
                out[at + 4 : at + 5, :] = jnp.sum(jnp.where(row == col, first_, 0.0), axis=0, keepdims=True)

            def both(*steps):
                def run():
                    for one in steps:
                        one()

                return run

            if f == 0:
                pl.when(sub == 0)(both(lambda: put(p_n, ()), lambda: put_one(t_n)))
                pl.when(sub == 1)(lambda: put(p_in, (1,)))
            elif f == 1:
                pl.when(sub == 0)(lambda: put(p_in, (0,)))
                pl.when(sub == 1)(both(lambda: put(p_s, ()), lambda: put_one(t_s)))
            else:
                kept, out_ = (p_w, t_w) if f == 2 else (p_e, t_e)
                pl.when(sub == 0)(lambda: put(kept, (0,)))
                pl.when(sub == 1)(both(lambda: put(kept, (1,)), lambda: put_two(out_, kept)))


def schur(order, inverse, couple, stiff, basis, loads, index):
    pkt = pltpu.HBM((PKT, NF), F32)
    pair = pltpu.HBM((2, PKT, NF), F32)
    one = jax.ShapeDtypeStruct((ONE, NF), F32)
    two = jax.ShapeDtypeStruct((TWO, NF), F32)
    return pl.pallas_call(
        schur_kernel,
        grid=(2, STEPS),
        in_specs=[
            pl.BlockSpec((None, None, 4, NF), lambda s, j: (s, 0, 0, 0)),
            pl.BlockSpec((None, None, CHUNK, NI), lambda s, j: (s, 0, j, 0)),
            pl.BlockSpec((None, None, NI, 4 * NF), lambda s, j: (s, 0, 0, 0)),
            pl.BlockSpec((None, None, 4, NF, NF), lambda s, j: (s, 0, 0, 0, 0)),
            pl.BlockSpec((None, None, NCOR, 4 * NF), lambda s, j: (s, 0, 0, 0)),
            pl.BlockSpec((None, None, 4, NF), lambda s, j: (s, 0, 0, 0)),
            pl.BlockSpec((None, 1, NCOR), lambda s, j: (s, 0, 0)),
        ],
        out_specs=[
            pl.BlockSpec((None, 10, NF, NF), lambda s, j: (s, 0, 0, 0)),
            pl.BlockSpec((2, PKT, NF), lambda s, j: (0, 0, 0)),
            pl.BlockSpec((PKT, NF), lambda s, j: (0, 0)),
            pl.BlockSpec((PKT, NF), lambda s, j: (0, 0)),
            pl.BlockSpec((2, PKT, NF), lambda s, j: (0, 0, 0)),
            pl.BlockSpec((2, PKT, NF), lambda s, j: (0, 0, 0)),
            pl.BlockSpec((ONE, NF), lambda s, j: (0, 0)),
            pl.BlockSpec((ONE, NF), lambda s, j: (0, 0)),
            pl.BlockSpec((TWO, NF), lambda s, j: (0, 0)),
            pl.BlockSpec((TWO, NF), lambda s, j: (0, 0)),
        ],
        out_shape=[jax.ShapeDtypeStruct((2, 10, NF, NF), BF16), pair, pkt, pkt, pair, pair, one, one, two, two],
        scratch_shapes=[
            pltpu.VMEM((4 * NF, NI), BF16),
            pltpu.VMEM((NI, 4 * NF), BF16),
            pltpu.VMEM((4, NF, NF), BF16),
        ],
        compiler_params=pltpu.CompilerParams(
            dimension_semantics=("arbitrary", "arbitrary"), vmem_limit_bytes=40 * 2**20
        ),
        cost_estimate=pl.CostEstimate(flops=16 * 10**9, transcendentals=0, bytes_accessed=32 * 2**20),
        name="schur",
    )(*(pltpu.with_memory_space_constraint(x, pltpu.HBM) for x in (order, inverse, couple, stiff, basis, loads, index)))


def spread_window(place, contributions):
    corner = iota((NCOR, 128), 0)
    lane = iota((NCOR, 128), 1)
    below = jnp.where(corner >= 12, 1, 0)
    inside = corner - 12 * below
    right = inside >= 6
    dof = inside - jnp.where(right, 6, 0)
    cols = [jnp.zeros((1, 128), F32) for _ in range(4)]
    for g, value in contributions.items():
        target = (2 * place[0] + GROUP_ROW[g] + below) * 6 + dof
        filled = jnp.where(lane == target, jnp.broadcast_to(value, (NCOR, 128)), 0.0)
        left = jnp.sum(jnp.where(right, 0.0, filled), axis=0, keepdims=True)
        both = jnp.sum(filled, axis=0, keepdims=True)
        cols[GROUP_COL[g]] = cols[GROUP_COL[g]] + left
        cols[GROUP_COL[g] + 1] = cols[GROUP_COL[g] + 1] + (both - left)
    return cols


def row_dot(matrix, row):
    return jnp.sum(matrix * row, axis=1, keepdims=True)


def face_kernel(
    place, live, h_in, h_n, h_s, h_w, h_e, q_n, q_s, q_w, q_e, finv, tmap, r_out, z_out, slots, send,
    a_hi, a_lo, x, p_in, p_n, p_s, p_w, p_e, sems
):
    sources = (h_in, h_n, h_s, h_w, h_e)
    targets = (p_in, p_n, p_s, p_w, p_e)
    copies = [pltpu.make_async_copy(sources[i], targets[i], sems.at[i]) for i in range(5)]
    for copy in copies:
        copy.start()
    for copy in copies:
        copy.wait()

    def kept(m):
        return (p_n, p_in.at[0], p_s, p_w.at[0], p_w.at[1], p_e.at[0], p_e.at[1])[m]

    def alive(m):
        return (live[0], 1.0, live[1], live[2], live[2], live[3], live[3])[m]

    def own_part(m, start_, count):
        return kept(m)[start_ : start_ + count, :]

    def other_part(m, start_, count):
        if m == 1:
            return p_in[1, NF + start_ : NF + start_ + count, :]
        if m in (0, 2):
            at = HALF + start_
            return (q_n if m == 0 else q_s)[at : at + count, :]
        side = q_w if m < 5 else q_e
        which = (m - 3) % 2
        at = NF + NCOR * which if start_ == 0 else NF + 2 * NCOR + 2 * which + start_ - NCOR
        return side[at : at + count, :]

    def one_square(q):
        row, col = iota((HALF, HALF), 0), iota((HALF, HALF), 1)
        square = q[0:HALF, 0:HALF]
        low = q[0:HALF, HALF:]
        turned = jnp.transpose(square)
        line = q[HALF + NCOR + 2 : HALF + NCOR + 3, 0:HALF]
        upper = jnp.where(row > col, square, jnp.where(row < col, turned, line))
        lower = jnp.where(row > col, turned, square)
        return jnp.concatenate(
            [jnp.concatenate([upper, jnp.transpose(low)], axis=1), jnp.concatenate([low, lower], axis=1)], axis=0
        )

    def two_squares(q):
        row, col = iota((NF, NF), 0), iota((NF, NF), 1)
        square = q[0:NF, :]
        turned = jnp.transpose(square)
        line = q[NF + 2 * NCOR + 4 : NF + 2 * NCOR + 5, :]
        return (
            jnp.where(row > col, square, jnp.where(row < col, turned, line)),
            jnp.where(row > col, turned, square),
        )

    others = (one_square(q_n), p_in[1, 0:NF, :], one_square(q_s), *two_squares(q_w), *two_squares(q_e))
    eye = jnp.where(iota((NF, NF), 0) == iota((NF, NF), 1), 1.0, 0.0)
    guess = []
    for m in range(7):
        full = own_part(m, 0, NF) + others[m]
        hi, lo = split2(full)
        a_hi[m] = hi
        a_lo[m] = lo
        size = jnp.max(jnp.sum(jnp.abs(full), axis=0, keepdims=True))
        scale = 1.9 / size
        guess.append(scale)
        x[m] = scale * (2.0 * eye - scale * full)

    def rough(state):
        count, _ = state
        worst = jnp.float32(0.0)
        for m in range(7):
            now = x[m]
            near = now.astype(BF16)
            left = eye - nn(a_hi[m], near)
            worst = jnp.maximum(worst, jnp.sum(left * left))
            x[m] = now + nn(near, left.astype(BF16))
        return count + 1, worst

    def rough_on(state):
        count, worst = state
        return jnp.logical_and(count < 24, jnp.logical_not(worst < 0.1))

    _, worst = lax.while_loop(rough_on, rough, (jnp.int32(0), jnp.float32(1e9)))
    fine_start = worst < 0.1

    @pl.when(jnp.logical_not(fine_start))
    def _():
        for m in range(7):
            x[m] = guess[m] * eye

    def fine(state):
        count, _ = state
        worst = jnp.float32(0.0)
        for m in range(7):
            now = x[m]
            hi, lo = split2(now)
            left = eye - (nn(a_hi[m], hi) + (nn(a_hi[m], lo) + nn(a_lo[m], hi)))
            worst = jnp.maximum(worst, jnp.sum(left * left))
            x[m] = now + nn(hi, left.astype(BF16))
        return count + 1, worst

    def fine_on(state):
        count, worst = state
        return jnp.logical_and(count < 60, jnp.logical_not(worst < 1e-3))

    lax.while_loop(fine_on, fine, (jnp.int32(0), jnp.float32(1e9)))

    gathered = {}

    def gather(g, value):
        gathered[g] = value if g not in gathered else gathered[g] + value

    rows_r = []
    rows_i = [None] * 8
    for m in range(7):
        inverse = x[m] * alive(m)
        finv[m] = inverse
        both = jnp.concatenate([own_part(m, NF, NCOR), other_part(m, 0, NCOR)], axis=0)
        b_hi, b_lo = split2(both)
        i_hi, i_lo = split2(inverse)
        lifted = nn(jnp.concatenate([b_hi, b_lo], axis=0), i_hi)
        mapped = lifted[:48] + lifted[48:] + nn(b_hi, i_lo)
        tmap[m] = mapped
        resid = alive(m) * (own_part(m, NF + NCOR, 1) + other_part(m, NCOR, 1))
        rows_r.append(resid)
        gather(GROUPS[m][0], row_dot(mapped[:NCOR], resid))
        if m == 1:
            gather(GROUPS[m][1], row_dot(mapped[NCOR:], resid))
        rows_i[GROUPS[m][0]] = own_part(m, NF + NCOR + 1, 1)[:, 0:128]
        rows_i[GROUPS[m][1]] = other_part(m, NCOR + 1, 1)[:, 0:128]
    resid = jnp.concatenate(rows_r + [jnp.zeros((1, NF), F32)], axis=0)
    r_out[...] = resid
    z_out[...] = face_apply(finv, resid)
    numbers = jnp.transpose(jnp.concatenate(rows_i, axis=0))[:NCOR, :]
    slots[...] = numbers
    sums = spread_window(place, gathered)
    upper = iota((NCOR, 1), 0) < 12
    named = {0: jnp.where(upper, numbers[:, 0:1] + 1.0, 0.0)}
    keep = jnp.logical_or(upper, place[0] == GRID_X - 1)
    named[1] = jnp.where(keep, numbers[:, 1:2] + 1.0, 0.0)
    names = spread_window(place, named)
    edge = jnp.where(place[1] == GRID_Y - 1, names[2], 0.0)
    send[...] = jnp.broadcast_to(jnp.concatenate([sums[1], sums[2], names[1], edge], axis=1), (DEV, 512))


def face_apply(finv, rows):
    turned = jnp.transpose(rows)
    outs = [jnp.sum(finv[m] * turned[:, m : m + 1], axis=0, keepdims=True) for m in range(7)]
    return jnp.concatenate(outs + [jnp.zeros((1, NF), F32)], axis=0)


def smem():
    return pl.BlockSpec(memory_space=pltpu.SMEM)


def vmem():
    return pl.BlockSpec(memory_space=pltpu.VMEM)


def faces(place, live, *packets):
    return pl.pallas_call(
        face_kernel,
        in_specs=[smem(), smem()] + [pl.BlockSpec(memory_space=pl.ANY)] * 5 + [vmem()] * 4,
        out_shape=[
            jax.ShapeDtypeStruct((7, NF, NF), F32),
            jax.ShapeDtypeStruct((7, 48, NF), F32),
            jax.ShapeDtypeStruct((8, NF), F32),
            jax.ShapeDtypeStruct((8, NF), F32),
            jax.ShapeDtypeStruct((NCOR, 8), F32),
            jax.ShapeDtypeStruct((DEV, 512), F32),
        ],
        scratch_shapes=[
            pltpu.VMEM((7, NF, NF), BF16),
            pltpu.VMEM((7, NF, NF), BF16),
            pltpu.VMEM((7, NF, NF), F32),
            pltpu.VMEM((2, PKT, NF), F32),
            pltpu.VMEM((PKT, NF), F32),
            pltpu.VMEM((PKT, NF), F32),
            pltpu.VMEM((2, PKT, NF), F32),
            pltpu.VMEM((2, PKT, NF), F32),
            pltpu.SemaphoreType.DMA((5,)),
        ],
        compiler_params=pltpu.CompilerParams(vmem_limit_bytes=16 * 2**20),
        cost_estimate=pl.CostEstimate(flops=5 * 10**9, transcendentals=0, bytes_accessed=10 * 2**20),
        name="faces",
    )(place, live, *packets)


def total_rows(got):
    total = got[0:GRID_Y, 0:512]
    for ix in range(1, GRID_X):
        total = total + got[ix * GRID_Y : (ix + 1) * GRID_Y, 0:512]
    return total


def owner_line(inverse, grid):
    partial = jnp.zeros((16, 128), F32)
    for col in range(1, 18):
        partial = partial + inverse[col] * grid[col : col + 1, :]
    column = jnp.sum(partial, axis=1, keepdims=True)
    return jnp.sum(jnp.where(iota((16, 128), 0) == iota((16, 128), 1), column, 0.0), axis=0, keepdims=True)


def start_kernel(got, columns, inverse, out, grid, table, padded):
    total = total_rows(got)
    grid[...] = jnp.zeros((VC, 128), F32)
    grid[1:17, :] = total[:, 0:128]
    grid[2:18, :] = grid[2:18, :] + total[:, 128:256]
    table[1:17, :] = total[:, 256:384]
    table[17:18, :] = total[GRID_Y - 1 : GRID_Y, 384:512]
    padded[...] = jnp.zeros((16, NCOARSE), F32)
    padded[0:OWN, :] = columns[...]
    lhs = jnp.concatenate(split3(padded[...]), axis=0)
    rows = iota((NCOARSE, 256), 0) + 1
    for pair in range(9):
        first_ = table[2 * pair + 1 : 2 * pair + 2, :]
        second_ = table[2 * pair + 2 : 2 * pair + 3, :] if pair < 8 else jnp.zeros((1, 128), F32)
        wanted = jnp.concatenate([first_, second_], axis=1).astype(jnp.int32)
        got_ = nn(lhs, (rows == wanted).astype(BF16))
        got_ = got_[0:16] + got_[16:32] + got_[32:48]
        inverse[2 * pair + 1] = got_[:, :128]
        if pair < 8:
            inverse[2 * pair + 2] = got_[:, 128:]
    for other in (0, *range(18, VC)):
        inverse[other] = jnp.zeros((16, 128), F32)
    out[...] = jnp.broadcast_to(owner_line(inverse, grid), (DEV, 128))


def start(got, columns):
    return pl.pallas_call(
        start_kernel,
        out_shape=[jax.ShapeDtypeStruct((VC, 16, 128), F32), jax.ShapeDtypeStruct((DEV, 128), F32)],
        scratch_shapes=[pltpu.VMEM((VC, 128), F32), pltpu.VMEM((VC, 128), F32), pltpu.VMEM((16, NCOARSE), F32)],
        compiler_params=pltpu.CompilerParams(vmem_limit_bytes=8 * 2**20),
        cost_estimate=pl.CostEstimate(flops=10**9, transcendentals=0, bytes_accessed=2**20),
        name="start",
    )(got, columns)


def owner_kernel(place, live, got, inverse, image, out, sums, grid):
    total = total_rows(got)
    grid[...] = jnp.zeros((VC, 128), F32)
    for vc in range(4):
        grid[vc : vc + GRID_Y, :] = grid[vc : vc + GRID_Y, :] + total[:, vc * 128 : (vc + 1) * 128]
    sums[...] = jnp.broadcast_to(jnp.sum(total[:, 0:128], axis=0, keepdims=True), (8, 128))
    out[:, 0:128] = jnp.broadcast_to(owner_line(inverse, grid), (DEV, 128))
    out[:, 128:] = jnp.zeros((DEV, 512), F32)
    post(place, live, image, out)


def owners(place, live, got, inverse, image):
    return pl.pallas_call(
        owner_kernel,
        in_specs=[smem(), smem()] + [vmem()] * 3,
        out_shape=[jax.ShapeDtypeStruct((DEV, 640), F32), jax.ShapeDtypeStruct((8, 128), F32)],
        scratch_shapes=[pltpu.VMEM((VC, 128), F32)],
        compiler_params=pltpu.CompilerParams(vmem_limit_bytes=6 * 2**20),
        cost_estimate=pl.CostEstimate(flops=10**6, transcendentals=0, bytes_accessed=2**20),
        name="owners",
    )(place, live, got, inverse, image)


def coarse_values(slots, coarse):
    lane = iota((NCOR, 128), 1).astype(F32)
    owner_rows = []
    places = []
    for g in range(8):
        number = slots[:, g : g + 1]
        owner = jnp.floor((number + 0.5) * (1.0 / OWN))
        places.append(number - OWN * owner)
        owner_rows.append(jnp.where(lane == owner, 1.0, 0.0))
    picked = lax.dot_general(
        jnp.concatenate(owner_rows, axis=0),
        coarse[:, 0:128],
        (((1,), (0,)), ((), ())),
        precision=HIGHEST,
        preferred_element_type=F32,
    )
    return [
        jnp.sum(jnp.where(lane == places[g], picked[g * NCOR : (g + 1) * NCOR], 0.0), axis=1, keepdims=True)
        for g in range(8)
    ]


def prolong(tmap, values):
    outs = []
    for m in range(7):
        column = jnp.concatenate([values[GROUPS[m][0]], values[GROUPS[m][1]]], axis=0)
        outs.append(jnp.sum(tmap[m] * column, axis=0, keepdims=True))
    return jnp.concatenate(outs + [jnp.zeros((1, NF), F32)], axis=0)


def subdomain_apply(s_ref, vector):
    turned = jnp.transpose(vector)
    rows = []
    for s in range(2):
        across = [None] * 4
        upright = [None] * 4
        for f in range(4):
            column = turned[:, FACE[s][f] : FACE[s][f] + 1]
            for g in range(f, 4):
                block = s_ref[s, BLOCK[f, g]].astype(F32)
                down = jnp.sum(block * column, axis=0, keepdims=True)
                across[g] = down if across[g] is None else across[g] + down
                if g > f:
                    m = FACE[s][g]
                    side = row_dot(block, vector[m : m + 1, :])
                    upright[f] = side if upright[f] is None else upright[f] + side
        columns = jnp.concatenate(
            [jnp.broadcast_to(upright[f], (NF, 128)) if f < 3 else jnp.zeros((NF, 128), F32) for f in range(4)], axis=1
        )
        lane_pick = jnp.concatenate([columns[:, f * 128 : f * 128 + 1] for f in range(4)] * 2, axis=1)
        flipped = jnp.transpose(lane_pick)
        for f in range(4):
            rows.append(across[f] + flipped[f : f + 1, :])
    return jnp.concatenate(rows, axis=0)


def restrict(place, tmap, image):
    gathered = {}

    def gather(g, value):
        gathered[g] = value if g not in gathered else gathered[g] + value

    for m in range(7):
        line = None
        for s in range(2):
            for f in range(4):
                if FACE[s][f] == m:
                    row = image[s * 4 + f : s * 4 + f + 1, :]
                    line = row if line is None else line + row
        gather(GROUPS[m][0], row_dot(tmap[m, 0:NCOR], line))
        gather(GROUPS[m][1], row_dot(tmap[m, NCOR:], line))
    return spread_window(place, gathered)


def post(place, live, image, send):
    me = place[0] * GRID_Y + place[1]

    def put(target, slot, row):
        at = pl.ds(target, 1)
        send[at, slot * 128 : slot * 128 + NF] = image[row : row + 1, :]

    @pl.when(live[0] > 0.0)
    def _():
        put(me - GRID_Y, 1, 0)

    @pl.when(live[1] > 0.0)
    def _():
        put(me + GRID_Y, 1, 5)

    @pl.when(live[2] > 0.0)
    def _():
        put(me - 1, 1, 2)
        put(me - 1, 3, 6)

    @pl.when(live[3] > 0.0)
    def _():
        put(me + 1, 1, 3)
        put(me + 1, 3, 7)


def meet(place, live, image, got):
    me = place[0] * GRID_Y + place[1]

    def read(source, slot, alive):
        at = jnp.clip(source, 0, DEV - 1)
        row = got[pl.ds(at, 1), slot * 128 : slot * 128 + NF]
        return jnp.where(alive > 0.0, row, 0.0)

    def mine(row):
        return image[row : row + 1, :]

    return jnp.concatenate(
        [
            live[0] * (mine(0) + read(me - GRID_Y, 1, live[0])),
            mine(1) + mine(4),
            live[1] * (mine(5) + read(me + GRID_Y, 1, live[1])),
            live[2] * (mine(2) + read(me - 1, 1, live[2])),
            live[2] * (mine(6) + read(me - 1, 3, live[2])),
            live[3] * (mine(3) + read(me + 1, 1, live[3])),
            live[3] * (mine(7) + read(me + 1, 3, live[3])),
            jnp.zeros((1, NF), F32),
        ],
        axis=0,
    )


def shared_dot(first, second):
    weight = jnp.where(iota((8, NF), 0) == 1, 1.0, 0.5)
    return jnp.sum(weight * first * second)


def sides(vector):
    return jnp.concatenate([vector[m : m + 1, :] for s in range(2) for m in FACE[s]], axis=0)


def tag(row, *scalars):
    lane = iota((1, 128), 1)
    for at, value in scalars:
        row = jnp.where(lane == at, value, row)
    return row


def first_kernel(place, live, s_ref, tmap, resid, smooth, slots, coarse, z_out, c_out, send):
    z = smooth[...] + prolong(tmap, coarse_values(slots, coarse))
    z_out[...] = z
    image = subdomain_apply(s_ref, z)
    c_out[...] = image
    cols = restrict(place, tmap, image)
    gamma = shared_dot(resid[...], z)
    delta = jnp.sum(sides(z) * image)
    cols[0] = tag(cols[0], (120, gamma), (121, delta))
    send[...] = jnp.broadcast_to(jnp.concatenate(cols, axis=1), (DEV, 512))


def first(place, live, *rest):
    return pl.pallas_call(
        first_kernel,
        in_specs=[smem(), smem()] + [vmem()] * 6,
        out_shape=[
            jax.ShapeDtypeStruct((8, NF), F32),
            jax.ShapeDtypeStruct((8, NF), F32),
            jax.ShapeDtypeStruct((DEV, 512), F32),
        ],
        compiler_params=pltpu.CompilerParams(vmem_limit_bytes=10 * 2**20),
        cost_estimate=pl.CostEstimate(flops=10**7, transcendentals=0, bytes_accessed=10 * 2**20),
        name="first",
    )(place, live, *rest)


def pick_lane(row, at):
    return jnp.sum(jnp.where(iota((1, 128), 1) == at, row, 0.0))


def second_kernel(place, live, s_ref, finv, tmap, resid, z_old, c_old, slots, sums, got, z_out, c_out, w_out, r_out, send):
    gamma = pick_lane(sums[0:1, :], 120)
    delta = pick_lane(sums[0:1, :], 121)
    alpha = gamma / delta
    w = meet(place, live, c_old, got)
    w_out[...] = w
    y = face_apply(finv, w) + prolong(tmap, coarse_values(slots, got))
    z = z_old[...] - alpha * y
    r = resid[...] - alpha * w
    z_out[...] = z
    r_out[...] = r
    image = subdomain_apply(s_ref, z)
    c_out[...] = image
    gamma_new = shared_dot(r, z)
    new_new = jnp.sum(sides(z) * image)
    old_new = jnp.sum(sides(z_old[...]) * image)
    new_old = jnp.sum(sides(z) * c_old[...])
    line = tag(
        jnp.zeros((1, 128), F32), (0, gamma_new), (1, new_new), (2, old_new), (3, new_old)
    )
    send[:, 0:128] = jnp.broadcast_to(line, (DEV, 128))
    send[:, 128:] = jnp.zeros((DEV, 512), F32)
    post(place, live, image, send)


def second(place, live, *rest):
    small = jax.ShapeDtypeStruct((8, NF), F32)
    return pl.pallas_call(
        second_kernel,
        in_specs=[smem(), smem()] + [vmem()] * 9,
        out_shape=[small, small, small, small, jax.ShapeDtypeStruct((DEV, 640), F32)],
        compiler_params=pltpu.CompilerParams(vmem_limit_bytes=14 * 2**20),
        cost_estimate=pl.CostEstimate(flops=10**7, transcendentals=0, bytes_accessed=12 * 2**20),
        name="second",
    )(place, live, *rest)


def last_kernel(place, live, z_old, w_old, z_new, c_new, resid, sums, got, x_out, r_out):
    line = jnp.sum(got[:, 0:128], axis=0, keepdims=True)
    gamma = pick_lane(sums[0:1, :], 120)
    delta = pick_lane(sums[0:1, :], 121)
    alpha = gamma / delta
    gamma_new = pick_lane(line, 0)
    beta = gamma_new / gamma
    curve = pick_lane(line, 1) + beta * (pick_lane(line, 2) + pick_lane(line, 3)) + beta * beta * delta
    alpha_new = gamma_new / curve
    w = meet(place, live, c_new[...], got)
    search = z_new[...] + beta * z_old[...]
    along = w + beta * w_old[...]
    x = sides(alpha * z_old[...] + alpha_new * search)
    r = sides(resid[...] - alpha_new * along)
    for s in range(2):
        x_out[s, 0] = x[4 * s : 4 * s + 4]
        r_out[s, 0] = r[4 * s : 4 * s + 4]


def last(place, live, *rest):
    out = jax.ShapeDtypeStruct((2, 1, 4, NF), F32)
    return pl.pallas_call(
        last_kernel,
        in_specs=[smem(), smem()] + [vmem()] * 7,
        out_shape=[out, out],
        compiler_params=pltpu.CompilerParams(vmem_limit_bytes=6 * 2**20),
        cost_estimate=pl.CostEstimate(flops=10**6, transcendentals=0, bytes_accessed=2**20),
        name="last",
    )(place, live, *rest)


def shift(value, axis, steps):
    count = lax.axis_size(axis)
    first_, last_ = max(0, -steps), min(count, count - steps)
    return lax.ppermute(value, axis, [(source, source + steps) for source in range(first_, last_)])


def exchange(packet):
    return lax.all_to_all(packet, GX_GY, 0, 0, tiled=True)


def shards(inverse, couple, stiff, basis, loads, order, corner_index, coarse_inverse):
    ix = lax.axis_index(GX)
    iy = lax.axis_index(GY)
    place = jnp.stack([ix, iy]).astype(jnp.int32)
    live = jnp.stack([ix > 0, ix < GRID_X - 1, iy > 0, iy < GRID_Y - 1]).astype(F32)
    s_full, p_in, p_n, p_s, p_w, p_e, t_n, t_s, t_w, t_e = schur(order, inverse, couple, stiff, basis, loads, corner_index)
    q_s = shift(t_n, GX, -1)
    q_n = shift(t_s, GX, 1)
    q_e = shift(t_w, GY, -1)
    q_w = shift(t_e, GY, 1)
    finv, tmap, resid, smooth, slots, send = faces(
        place, live, *(pltpu.with_memory_space_constraint(p, pltpu.HBM) for p in (p_in, p_n, p_s, p_w, p_e)), q_n, q_s, q_w, q_e
    )
    coarse, values = start(exchange(send), jnp.transpose(coarse_inverse))
    z0, c0, send = first(place, live, s_full, tmap, resid, smooth, slots, exchange(values))
    send, sums = owners(place, live, exchange(send), coarse, c0)
    z1, c1, w0, r1, send = second(place, live, s_full, finv, tmap, resid, z0, c0, slots, sums, exchange(send))
    return tuple(last(place, live, z0, w0, z1, c1, r1, sums, exchange(send)))


def solution(mesh):
    torus = Mesh(mesh.devices.reshape(4, 2, 4, 2, 2), GX_GY)
    in_specs = (
        P(GX, GY, None, None),
        P(GX, GY, None, None),
        P(GX, GY, None, None, None),
        P(GX, GY, None, None),
        P(GX, GY, None, None),
        P(GX, GY, None, None),
        P(GX, GY, None),
        P(None, GX_GY),
    )
    out_specs = (P(GX, GY, None, None), P(GX, GY, None, None))
    return jax.shard_map(shards, mesh=torus, in_specs=in_specs, out_specs=out_specs, check_vma=False)
```

time: 189 us -> 156 us (0.83)
  starting transfers between devices: 40.6 us -> 12.3 us
  local copies, waits for them, and re-layouts: 21.1 us -> 1.3 us
  blocking collectives: 64.4 us -> 80.9 us
  waiting for transfers between devices: 8.41 us -> 10.4 us
  Pallas kernels: 51.5 us -> 49.6 us
    all_to_all x2 -> x0, starting transfers between devices: 28.6 us -> none  [exchange(): return lax.all_to_all(packet, GX_GY, 0, 0, tiled=True)]
    unnamed x44 -> x6, local copies, waits for them, and re-layouts: 18.4 us -> 0.08 us
    all_to_all x4 -> x5, blocking collectives: 64.4 us -> 80.9 us  [exchange(): return lax.all_to_all(packet, GX_GY, 0, 0, tiled=True)]
    ppermute x4, waiting for transfers between devices: 0.01 us -> 10.4 us  [shift(): lax.ppermute(value, axis, [(source, source + steps) for source in range(f...]
    all_to_all x2 -> x0, waiting for transfers between devices: 8.4 us -> none  [exchange(): return lax.all_to_all(packet, GX_GY, 0, 0, tiled=True)]
    pallas_call x5 -> x4, Pallas kernels: 20.8 us -> 19.7 us  [the longest x1 13.8 us: faces(): pl.pallas_call(face_kernel, in_specs=[smem(), smem()] + [pl.BlockSpec(mem...]
  transfers between devices with their start and end apart: 6 -> 4, of which waited for: 1 -> 2; matrix products, arithmetic and copies ran while one was open for 1% -> 0% of each run, Pallas kernels for 7% -> 0%
where the time goes in v2:
time: 156 us; the launch traced here: 155 us
  blocking collectives  80.9 us (52%)
  Pallas kernels  49.6 us (32%)
  starting transfers between devices  12.3 us (8%)
  waiting for transfers between devices  10.4 us (7%)
    all_to_all x5, blocking collectives, exchange(): return lax.all_to_all(packet, GX_GY, 0, 0, tiled=True)  80.9 us
    pallas_call x1, Pallas kernels, schur(): pl.pallas_call(schur_kernel, grid=(2, STEPS), in_specs=[pl.BlockSpec((Non...  25.8 us
    pallas_call x1, Pallas kernels, faces(): pl.pallas_call(face_kernel, in_specs=[smem(), smem()] + [pl.BlockSpec(mem...  13.8 us
    ppermute x4, starting transfers between devices, shift(): lax.ppermute(value, axis, [(source, source + steps) for source in range(f...  12.3 us
    ppermute x4, waiting for transfers between devices, shift(): lax.ppermute(value, axis, [(source, source + steps) for source in range(f...  10.4 us
    pallas_call x1, Pallas kernels, second(): pl.pallas_call(second_kernel, in_specs=[smem(), smem()] + [vmem()] * 9, o...  3.71 us
  transfers between devices with their start and end apart: 4, of which 2 were waited for; matrix products, arithmetic and copies ran while one was open for 0% of the time, Pallas kernels for 0%

profile of v2, /device:TPU:1, one launch (start us, length us, event | category | flops | bytes accessed | tf_op | source)
XLA Modules:
  0.0 155.5 jit_solution(6558945810346296627)
XLA Ops:
  0.6 25.8 %schur.1 = (bf16[2,10,256,256]{3,2,1,0:T(8,128)(2,1)S(1)}, f32[2,288,256]{2,1,0:T(8,128)}, f32[288,256]{1,0:T(8,128)}, f32[288,256]{1,0:T(8,128)}, f32[2,288,256...) custom-call(s32[2,1,4,256]{3,2,1,0:T(4,128)} %order.1, ...), custom_call_target="tpu_custom_call" | custom-call | flops 16000000000 | bytes 33554432 | tf_op jit(solution)/shard_map/schur/pallas_call | solution.py:154
  26.5 4.6 %collective-permute-start.2 = (f32[312,256]{1,0:T(8,128)}, f32[312,256]{1,0:T(8,128)S(1)}, u32[]{:S(2)}, u32[]{:S(2)}) collective-permute-start(f32[312,256]{1,0:T(8,128)} %get-tuple-element.38), channel_id=1, source_target_pairs={{0,1},{1,2},{2,3},{3,4},{4,5},{5,6},{6,7},{7,8},{8,9},{9,10},{10,1... | collective-permute-start | bytes 958472 | tf_op jit(solution)/shard_map/ppermute | solution.py:720
  31.1 1.9 %collective-permute-start.3 = (f32[312,256]{1,0:T(8,128)}, f32[312,256]{1,0:T(8,128)S(1)}, u32[]{:S(2)}, u32[]{:S(2)}) collective-permute-start(f32[312,256]{1,0:T(8,128)} %get-tuple-element.39), channel_id=1, source_target_pairs={{1,0},{2,1},{3,2},{4,3},{5,4},{6,5},{7,6},{8,7},{9,8},{10,9},{11,1... | collective-permute-start | bytes 958472 | tf_op jit(solution)/shard_map/ppermute | solution.py:720
  33.0 4.5 %collective-permute-start = (f32[160,256]{1,0:T(8,128)}, f32[160,256]{1,0:T(8,128)S(1)}, u32[]{:S(2)}, u32[]{:S(2)}) collective-permute-start(f32[160,256]{1,0:T(8,128)} %get-tuple-element.36), channel_id=1, source_target_pairs={{0,16},{16,32},{32,48},{48,64},{64,80},{80,96},{96,112},{1,17},{17... | collective-permute-start | bytes 491528 | tf_op jit(solution)/shard_map/ppermute | solution.py:720
  37.5 1.3 collective-permute-start.1
  38.8 0.1 pad_add_fusion.place
  38.9 0.1 add_convert_fusion.live
  39.0 4.3 %collective-permute-done.q_n = f32[160,256]{1,0:T(8,128)S(1)} collective-permute-done((f32[160,256]{1,0:T(8,128)}, f32[160,256]{1,0:T(8,128)S(1)}, u32[]{:S(2)}, u32[]{:S(2)}) %collective-permute-start) | collective-permute-done | bytes 163872 | tf_op jit(solution)/shard_map/ppermute | solution.py:720
  43.3 6.1 %collective-permute-done.1.q_s = f32[160,256]{1,0:T(8,128)} collective-permute-done((f32[160,256]{1,0:T(8,128)}, f32[160,256]{1,0:T(8,128)}, u32[]{:S(2)}, u32[]{:S(2)}) %collective-permute-start.1) | collective-permute-done | bytes 163872 | tf_op jit(solution)/shard_map/ppermute | solution.py:720
  49.4 0.0 collective-permute-done.2.q_w
  49.4 0.0 collective-permute-done.3.q_e
  49.4 0.0 copy-start
  49.4 13.8 %faces.1 = (f32[7,256,256]{2,1,0:T(8,128)S(1)}, f32[7,48,256]{2,1,0:T(8,128)S(1)}, f32[8,256]{1,0:T(8,128)S(1)}, f32[8,256]{1,0:T(8,128)S(1)}, f32[24,8]{1,0:T(8,128)S(1)}, /*index=5*/f32[128,512]{1,0:T(8,128)S(1)}) custom-call(s32[2]{0:T(128)S(1)} %pad_add_fusion.place, f32[4]{0:T(128)S(1)} %add_convert_fusion.live, f32[2,288,256]{2,1,0:T(8,128)} %get-tuple-element.31.h_in, ...), custom_call_target="tpu_custom_call" | custom-call | flops 5000000000 | bytes 10485760 | tf_op jit(solution)/shard_map/faces/pallas_call | solution.py:374
  63.2 0.3 copy.10
  63.5 20.4 %all_to_all.55 = f32[128,1,512]{2,1,0:T(1,128)S(1)} all-to-all(f32[128,1,512]{2,1,0:T(1,128)S(1)} %copy.10), channel_id=1, replica_groups=mesh['gx_0'=4,'gx_1'=2,'gy_0'=4,'gy_1'=2,'gy_2'=2] {'gx_0','gx_1','gy_0'..., dimensions={0} | all-to-all | bytes 524288 | tf_op jit(solution)/shard_map/all_to_all | solution.py:724
  83.9 0.0 copy-done
  83.9 1.5 start.1
  85.4 13.6 %all_to_all.56 = f32[128,1,128]{2,1,0:T(1,128)S(1)} all-to-all(f32[128,1,128]{2,1,0:T(1,128)S(1)} %bitcast.36), channel_id=1, replica_groups=mesh['gx_0'=4,'gx_1'=2,'gy_0'=4,'gy_1'=2,'gy_2'=2] {'gx_0','gx_1','gy_0'..., dimensions={0} | all-to-all | bytes 131072 | tf_op jit(solution)/shard_map/all_to_all | solution.py:724
  99.0 2.7 %first.1 = (f32[8,256]{1,0:T(8,128)S(1)}, f32[8,256]{1,0:T(8,128)S(1)}, f32[128,512]{1,0:T(8,128)S(1)}) custom-call(s32[2]{0:T(128)S(1)} %pad_add_fusion.place, f32[4]{0:T(128)S(1)} %add_convert_fusion.live, bf16[2,10,256,256]{3,2,1,0:T(8,128)(2,1)S(1)} %get-tuple-element.30.s_ref, f32[7,48,256]{2,1,0:T(8,128)S(1)} %get-tuple-element.40.tmap, ...), custom_call_target="tpu_custom_call" | custom-call | flops 10000000 | bytes 10485760 | tf_op jit(solution)/shard_map/first/pallas_call | solution.py:631
  101.7 0.3 copy.12
  102.0 15.4 %all_to_all.57 = f32[128,1,512]{2,1,0:T(1,128)S(1)} all-to-all(f32[128,1,512]{2,1,0:T(1,128)S(1)} %copy.12), channel_id=1, replica_groups=mesh['gx_0'=4,'gx_1'=2,'gy_0'=4,'gy_1'=2,'gy_2'=2] {'gx_0','gx_1','gy_0'..., dimensions={0} | all-to-all | bytes 524288 | tf_op jit(solution)/shard_map/all_to_all | solution.py:724
  117.4 0.7 owners.1
  118.1 0.3 copy.13
  118.4 15.8 %all_to_all.58 = f32[128,1,640]{2,1,0:T(1,128)S(1)} all-to-all(f32[128,1,640]{2,1,0:T(1,128)S(1)} %copy.13), channel_id=1, replica_groups=mesh['gx_0'=4,'gx_1'=2,'gy_0'=4,'gy_1'=2,'gy_2'=2] {'gx_0','gx_1','gy_0'..., dimensions={0} | all-to-all | bytes 655360 | tf_op jit(solution)/shard_map/all_to_all | solution.py:724
  134.2 3.7 %second.1 = (f32[8,256]{1,0:T(8,128)S(1)}, f32[8,256]{1,0:T(8,128)S(1)}, f32[8,256]{1,0:T(8,128)S(1)}, f32[8,256]{1,0:T(8,128)S(1)}, f32[128,640]{1,0:T(8,128)S(1)}) custom-call(s32[2]{0:T(128)S(1)} %pad_add_fusion.place, f32[4]{0:T(128)S(1)} %add_convert_fusion.live, bf16[2,10,256,256]{3,2,1,0:T(8,128)(2,1)S(1)} %get-tuple-element.30.s_ref, ...), custom_call_target="tpu_custom_call" | custom-call | flops 10000000 | bytes 12582912 | tf_op jit(solution)/shard_map/second/pallas_call | solution.py:676
  137.9 0.3 copy.14
  138.3 15.8 %all_to_all.59 = f32[128,1,640]{2,1,0:T(1,128)S(1)} all-to-all(f32[128,1,640]{2,1,0:T(1,128)S(1)} %copy.14), channel_id=1, replica_groups=mesh['gx_0'=4,'gx_1'=2,'gy_0'=4,'gy_1'=2,'gy_2'=2] {'gx_0','gx_1','gy_0'..., dimensions={0} | all-to-all | bytes 655360 | tf_op jit(solution)/shard_map/all_to_all | solution.py:724
  154.1 1.4 last.1
  (4 shorter events, 0.1 us)
Async XLA Ops:
  26.5 22.9 %collective-permute-start.2 = (f32[312,256]{1,0:T(8,128)}, f32[312,256]{1,0:T(8,128)S(1)}, u32[]{:S(2)}, u32[]{:S(2)}) collective-permute-start(f32[312,256]{1,0:T(8,128)} %get-tuple-element.38), channel_id=1, source_target_pairs={{0,1},{1,2},{2,3},{3,4},{4,5},{5,6},{6,7},{7,8},{8,9},{9,10},{10,1... | collective-permute-start | bytes 958472 | tf_op jit(solution)/shard_map/ppermute | solution.py:720
  31.1 18.4 %collective-permute-start.3 = (f32[312,256]{1,0:T(8,128)}, f32[312,256]{1,0:T(8,128)S(1)}, u32[]{:S(2)}, u32[]{:S(2)}) collective-permute-start(f32[312,256]{1,0:T(8,128)} %get-tuple-element.39), channel_id=1, source_target_pairs={{1,0},{2,1},{3,2},{4,3},{5,4},{6,5},{7,6},{8,7},{9,8},{10,9},{11,1... | collective-permute-start | bytes 958472 | tf_op jit(solution)/shard_map/ppermute | solution.py:720
  33.0 10.3 %collective-permute-start = (f32[160,256]{1,0:T(8,128)}, f32[160,256]{1,0:T(8,128)S(1)}, u32[]{:S(2)}, u32[]{:S(2)}) collective-permute-start(f32[160,256]{1,0:T(8,128)} %get-tuple-element.36), channel_id=1, source_target_pairs={{0,16},{16,32},{32,48},{48,64},{64,80},{80,96},{96,112},{1,17},{17... | collective-permute-start | bytes 491528 | tf_op jit(solution)/shard_map/ppermute | solution.py:720
  37.5 11.9 %collective-permute-start.1 = (f32[160,256]{1,0:T(8,128)}, f32[160,256]{1,0:T(8,128)}, u32[]{:S(2)}, u32[]{:S(2)}) collective-permute-start(f32[160,256]{1,0:T(8,128)} %get-tuple-element.37), channel_id=1, source_target_pairs={{16,0},{32,16},{48,32},{64,48},{80,64},{96,80},{112,96},{17,1},{33... | collective-permute-start | bytes 491528 | tf_op jit(solution)/shard_map/ppermute | solution.py:720
  49.4 34.5 %copy-start = (f32[1792,14]{0,1:T(8,128)S(1)}, f32[1792,14]{0,1:T(8,128)}, u32[]{:S(2)}) copy-start(f32[1792,14]{0,1:T(8,128)} %param.15) | copy-start | bytes 301060

commit v3 on v2

--- a/solution.py
+++ b/solution.py
@@ -189,17 +189,17 @@
     )(*(pltpu.with_memory_space_constraint(x, pltpu.HBM) for x in (order, inverse, couple, stiff, basis, loads, index)))
 
 
-def spread_window(place, contributions):
-    corner = iota((NCOR, 128), 0)
-    lane = iota((NCOR, 128), 1)
+def spread_window(contributions):
+    corner = iota((NCOR, 32), 0)
+    lane = iota((NCOR, 32), 1)
     below = jnp.where(corner >= 12, 1, 0)
     inside = corner - 12 * below
     right = inside >= 6
     dof = inside - jnp.where(right, 6, 0)
-    cols = [jnp.zeros((1, 128), F32) for _ in range(4)]
+    cols = [jnp.zeros((1, 32), F32) for _ in range(4)]
     for g, value in contributions.items():
-        target = (2 * place[0] + GROUP_ROW[g] + below) * 6 + dof
-        filled = jnp.where(lane == target, jnp.broadcast_to(value, (NCOR, 128)), 0.0)
+        target = (GROUP_ROW[g] + 1 + below) * 6 + dof
+        filled = jnp.where(lane == target, jnp.broadcast_to(value, (NCOR, 32)), 0.0)
         left = jnp.sum(jnp.where(right, 0.0, filled), axis=0, keepdims=True)
         both = jnp.sum(filled, axis=0, keepdims=True)
         cols[GROUP_COL[g]] = cols[GROUP_COL[g]] + left
@@ -220,8 +220,6 @@
     copies = [pltpu.make_async_copy(sources[i], targets[i], sems.at[i]) for i in range(5)]
     for copy in copies:
         copy.start()
-    for copy in copies:
-        copy.wait()
 
     def kept(m):
         return (p_n, p_in.at[0], p_s, p_w.at[0], p_w.at[1], p_e.at[0], p_e.at[1])[m]
@@ -265,11 +263,17 @@
             jnp.where(row > col, turned, square),
         )
 
-    others = (one_square(q_n), p_in[1, 0:NF, :], one_square(q_s), *two_squares(q_w), *two_squares(q_e))
+    received = {0: one_square(q_n), 2: one_square(q_s)}
+    received[3], received[4] = two_squares(q_w)
+    received[5], received[6] = two_squares(q_e)
+    for m, block in received.items():
+        x[m] = block
+    for copy in copies:
+        copy.wait()
     eye = jnp.where(iota((NF, NF), 0) == iota((NF, NF), 1), 1.0, 0.0)
     guess = []
     for m in range(7):
-        full = own_part(m, 0, NF) + others[m]
+        full = own_part(m, 0, NF) + (p_in[1, 0:NF, :] if m == 1 else x[m])
         hi, lo = split2(full)
         a_hi[m] = hi
         a_lo[m] = lo
@@ -346,14 +350,14 @@
     z_out[...] = face_apply(finv, resid)
     numbers = jnp.transpose(jnp.concatenate(rows_i, axis=0))[:NCOR, :]
     slots[...] = numbers
-    sums = spread_window(place, gathered)
+    sums = spread_window(gathered)
     upper = iota((NCOR, 1), 0) < 12
     named = {0: jnp.where(upper, numbers[:, 0:1] + 1.0, 0.0)}
     keep = jnp.logical_or(upper, place[0] == GRID_X - 1)
     named[1] = jnp.where(keep, numbers[:, 1:2] + 1.0, 0.0)
-    names = spread_window(place, named)
+    names = spread_window(named)
     edge = jnp.where(place[1] == GRID_Y - 1, names[2], 0.0)
-    send[...] = jnp.broadcast_to(jnp.concatenate([sums[1], sums[2], names[1], edge], axis=1), (DEV, 512))
+    send[...] = jnp.broadcast_to(jnp.concatenate([sums[1], sums[2], names[1], edge], axis=1), (DEV, 128))
 
 
 def face_apply(finv, rows):
@@ -380,7 +384,7 @@
             jax.ShapeDtypeStruct((8, NF), F32),
             jax.ShapeDtypeStruct((8, NF), F32),
             jax.ShapeDtypeStruct((NCOR, 8), F32),
-            jax.ShapeDtypeStruct((DEV, 512), F32),
+            jax.ShapeDtypeStruct((DEV, 128), F32),
         ],
         scratch_shapes=[
             pltpu.VMEM((7, NF, NF), BF16),
@@ -399,11 +403,16 @@
     )(place, live, *packets)
 
 
-def total_rows(got):
-    total = got[0:GRID_Y, 0:512]
-    for ix in range(1, GRID_X):
-        total = total + got[ix * GRID_Y : (ix + 1) * GRID_Y, 0:512]
-    return total
+def total_columns(got):
+    lane = iota((GRID_Y, 128), 1)
+    totals = [None] * 4
+    for ix in range(GRID_X):
+        part = got[ix * GRID_Y : (ix + 1) * GRID_Y, :]
+        for v in range(4):
+            inside = jnp.logical_and(lane >= 32 * v, lane < 32 * v + 30)
+            moved = pltpu.roll(jnp.where(inside, part, 0.0), (12 * ix - 6 - 32 * v) % 128, 1)
+            totals[v] = moved if totals[v] is None else totals[v] + moved
+    return totals
 
 
 def owner_line(inverse, grid):
@@ -415,12 +424,12 @@
 
 
 def start_kernel(got, columns, inverse, out, grid, table, padded):
-    total = total_rows(got)
+    totals = total_columns(got)
     grid[...] = jnp.zeros((VC, 128), F32)
-    grid[1:17, :] = total[:, 0:128]
-    grid[2:18, :] = grid[2:18, :] + total[:, 128:256]
-    table[1:17, :] = total[:, 256:384]
-    table[17:18, :] = total[GRID_Y - 1 : GRID_Y, 384:512]
+    grid[1:17, :] = totals[0]
+    grid[2:18, :] = grid[2:18, :] + totals[1]
+    table[1:17, :] = totals[2]
+    table[17:18, :] = totals[3][GRID_Y - 1 : GRID_Y, :]
     padded[...] = jnp.zeros((16, NCOARSE), F32)
     padded[0:OWN, :] = columns[...]
     lhs = jnp.concatenate(split3(padded[...]), axis=0)
@@ -451,11 +460,11 @@
 
 
 def owner_kernel(place, live, got, inverse, image, out, sums, grid):
-    total = total_rows(got)
+    totals = total_columns(got)
     grid[...] = jnp.zeros((VC, 128), F32)
     for vc in range(4):
-        grid[vc : vc + GRID_Y, :] = grid[vc : vc + GRID_Y, :] + total[:, vc * 128 : (vc + 1) * 128]
-    sums[...] = jnp.broadcast_to(jnp.sum(total[:, 0:128], axis=0, keepdims=True), (8, 128))
+        grid[vc : vc + GRID_Y, :] = grid[vc : vc + GRID_Y, :] + totals[vc]
+    sums[...] = jnp.broadcast_to(jnp.sum(got[...], axis=0, keepdims=True), (8, 128))
     out[:, 0:128] = jnp.broadcast_to(owner_line(inverse, grid), (DEV, 128))
     out[:, 128:] = jnp.zeros((DEV, 512), F32)
     post(place, live, image, out)
@@ -529,7 +538,7 @@
     return jnp.concatenate(rows, axis=0)
 
 
-def restrict(place, tmap, image):
+def restrict(tmap, image):
     gathered = {}
 
     def gather(g, value):
@@ -544,7 +553,7 @@
                     line = row if line is None else line + row
         gather(GROUPS[m][0], row_dot(tmap[m, 0:NCOR], line))
         gather(GROUPS[m][1], row_dot(tmap[m, NCOR:], line))
-    return spread_window(place, gathered)
+    return spread_window(gathered)
 
 
 def post(place, live, image, send):
@@ -620,11 +629,11 @@
     z_out[...] = z
     image = subdomain_apply(s_ref, z)
     c_out[...] = image
-    cols = restrict(place, tmap, image)
+    cols = restrict(tmap, image)
     gamma = shared_dot(resid[...], z)
     delta = jnp.sum(sides(z) * image)
-    cols[0] = tag(cols[0], (120, gamma), (121, delta))
-    send[...] = jnp.broadcast_to(jnp.concatenate(cols, axis=1), (DEV, 512))
+    line = tag(jnp.concatenate(cols, axis=1), (30, gamma), (31, delta))
+    send[...] = jnp.broadcast_to(line, (DEV, 128))
 
 
 def first(place, live, *rest):
@@ -634,7 +643,7 @@
         out_shape=[
             jax.ShapeDtypeStruct((8, NF), F32),
             jax.ShapeDtypeStruct((8, NF), F32),
-            jax.ShapeDtypeStruct((DEV, 512), F32),
+            jax.ShapeDtypeStruct((DEV, 128), F32),
         ],
         compiler_params=pltpu.CompilerParams(vmem_limit_bytes=10 * 2**20),
         cost_estimate=pl.CostEstimate(flops=10**7, transcendentals=0, bytes_accessed=10 * 2**20),
@@ -647,8 +656,8 @@
 
 
 def second_kernel(place, live, s_ref, finv, tmap, resid, z_old, c_old, slots, sums, got, z_out, c_out, w_out, r_out, send):
-    gamma = pick_lane(sums[0:1, :], 120)
-    delta = pick_lane(sums[0:1, :], 121)
+    gamma = pick_lane(sums[0:1, :], 30)
+    delta = pick_lane(sums[0:1, :], 31)
     alpha = gamma / delta
     w = meet(place, live, c_old, got)
     w_out[...] = w
@@ -685,8 +694,8 @@
 
 def last_kernel(place, live, z_old, w_old, z_new, c_new, resid, sums, got, x_out, r_out):
     line = jnp.sum(got[:, 0:128], axis=0, keepdims=True)
-    gamma = pick_lane(sums[0:1, :], 120)
-    delta = pick_lane(sums[0:1, :], 121)
+    gamma = pick_lane(sums[0:1, :], 30)
+    delta = pick_lane(sums[0:1, :], 31)
     alpha = gamma / delta
     gamma_new = pick_lane(line, 0)
     beta = gamma_new / gamma

time: 156 us -> 152 us (0.974)
  blocking collectives: 80.9 us -> 78.3 us
    all_to_all x5, blocking collectives: 80.9 us -> 78.3 us  [exchange(): return lax.all_to_all(packet, GX_GY, 0, 0, tiled=True)]
where the time goes in v3:
time: 152 us
  blocking collectives  78.3 us (52%)
  Pallas kernels  49.5 us (33%)
  starting transfers between devices  12.3 us (8%)
  waiting for transfers between devices  10.4 us (7%)
    all_to_all x5, blocking collectives, exchange(): return lax.all_to_all(packet, GX_GY, 0, 0, tiled=True)  78.3 us
    pallas_call x1, Pallas kernels, schur(): pl.pallas_call(schur_kernel, grid=(2, STEPS), in_specs=[pl.BlockSpec((Non...  25.8 us
    pallas_call x1, Pallas kernels, faces(): pl.pallas_call(face_kernel, in_specs=[smem(), smem()] + [pl.BlockSpec(mem...  13.5 us
    ppermute x4, starting transfers between devices, shift(): lax.ppermute(value, axis, [(source, source + steps) for source in range(f...  12.3 us
    ppermute x4, waiting for transfers between devices, shift(): lax.ppermute(value, axis, [(source, source + steps) for source in range(f...  10.4 us
    pallas_call x1, Pallas kernels, second(): pl.pallas_call(second_kernel, in_specs=[smem(), smem()] + [vmem()] * 9, o...  3.67 us
  transfers between devices with their start and end apart: 4, of which 2 were waited for; matrix products, arithmetic and copies ran while one was open for 0% of the time, Pallas kernels for 0%

profile of v3, /device:TPU:1, one launch (start us, length us, event | category | flops | bytes accessed | tf_op | source)
XLA Modules:
  0.0 152.1 jit_solution(2366176149613831506)
XLA Ops:
  0.6 25.8 %schur.1 = (bf16[2,10,256,256]{3,2,1,0:T(8,128)(2,1)S(1)}, f32[2,288,256]{2,1,0:T(8,128)}, f32[288,256]{1,0:T(8,128)}, f32[288,256]{1,0:T(8,128)}, f32[2,288,256...) custom-call(s32[2,1,4,256]{3,2,1,0:T(4,128)} %order.1, ...), custom_call_target="tpu_custom_call" | custom-call | flops 16000000000 | bytes 33554432 | tf_op jit(solution)/shard_map/schur/pallas_call | solution.py:154
  26.5 4.6 %collective-permute-start.2 = (f32[312,256]{1,0:T(8,128)}, f32[312,256]{1,0:T(8,128)S(1)}, u32[]{:S(2)}, u32[]{:S(2)}) collective-permute-start(f32[312,256]{1,0:T(8,128)} %get-tuple-element.38), channel_id=1, source_target_pairs={{0,1},{1,2},{2,3},{3,4},{4,5},{5,6},{6,7},{7,8},{8,9},{9,10},{10,1... | collective-permute-start | bytes 958472 | tf_op jit(solution)/shard_map/ppermute | solution.py:729
  31.1 1.9 %collective-permute-start.3 = (f32[312,256]{1,0:T(8,128)}, f32[312,256]{1,0:T(8,128)S(1)}, u32[]{:S(2)}, u32[]{:S(2)}) collective-permute-start(f32[312,256]{1,0:T(8,128)} %get-tuple-element.39), channel_id=1, source_target_pairs={{1,0},{2,1},{3,2},{4,3},{5,4},{6,5},{7,6},{8,7},{9,8},{10,9},{11,1... | collective-permute-start | bytes 958472 | tf_op jit(solution)/shard_map/ppermute | solution.py:729
  33.0 4.5 %collective-permute-start = (f32[160,256]{1,0:T(8,128)}, f32[160,256]{1,0:T(8,128)S(1)}, u32[]{:S(2)}, u32[]{:S(2)}) collective-permute-start(f32[160,256]{1,0:T(8,128)} %get-tuple-element.36), channel_id=1, source_target_pairs={{0,16},{16,32},{32,48},{48,64},{64,80},{80,96},{96,112},{1,17},{17... | collective-permute-start | bytes 491528 | tf_op jit(solution)/shard_map/ppermute | solution.py:729
  37.5 1.3 collective-permute-start.1
  38.8 0.1 pad_add_fusion.place
  38.9 0.1 add_convert_fusion.live
  39.0 4.3 %collective-permute-done.q_n = f32[160,256]{1,0:T(8,128)S(1)} collective-permute-done((f32[160,256]{1,0:T(8,128)}, f32[160,256]{1,0:T(8,128)S(1)}, u32[]{:S(2)}, u32[]{:S(2)}) %collective-permute-start) | collective-permute-done | bytes 163872 | tf_op jit(solution)/shard_map/ppermute | solution.py:729
  43.3 6.1 %collective-permute-done.1.q_s = f32[160,256]{1,0:T(8,128)} collective-permute-done((f32[160,256]{1,0:T(8,128)}, f32[160,256]{1,0:T(8,128)}, u32[]{:S(2)}, u32[]{:S(2)}) %collective-permute-start.1) | collective-permute-done | bytes 163872 | tf_op jit(solution)/shard_map/ppermute | solution.py:729
  49.4 0.0 collective-permute-done.2.q_w
  49.4 0.0 collective-permute-done.3.q_e
  49.4 0.0 copy-start
  49.4 13.5 %faces.1 = (f32[7,256,256]{2,1,0:T(8,128)S(1)}, f32[7,48,256]{2,1,0:T(8,128)S(1)}, f32[8,256]{1,0:T(8,128)S(1)}, f32[8,256]{1,0:T(8,128)S(1)}, f32[24,8]{1,0:T(8,128)S(1)}, /*index=5*/f32[128,128]{1,0:T(8,128)S(1)}) custom-call(s32[2]{0:T(128)S(1)} %pad_add_fusion.place, f32[4]{0:T(128)S(1)} %add_convert_fusion.live, f32[2,288,256]{2,1,0:T(8,128)} %get-tuple-element.31.h_in, ...), custom_call_target="tpu_custom_call" | custom-call | flops 5000000000 | bytes 10485760 | tf_op jit(solution)/shard_map/faces/pallas_call | solution.py:378
  63.0 18.8 %all_to_all.55 = f32[128,1,128]{2,1,0:T(1,128)S(1)} all-to-all(f32[128,1,128]{2,1,0:T(1,128)S(1)} %bitcast.33), channel_id=1, replica_groups=mesh['gx_0'=4,'gx_1'=2,'gy_0'=4,'gy_1'=2,'gy_2'=2] {'gx_0','gx_1','gy_0'..., dimensions={0} | all-to-all | bytes 131072 | tf_op jit(solution)/shard_map/all_to_all | solution.py:733
  81.8 0.0 copy-done
  81.8 1.6 %start.1 = (f32[24,16,128]{2,1,0:T(8,128)S(1)}, f32[128,128]{1,0:T(8,128)S(1)}) custom-call(f32[128,128]{1,0:T(8,128)S(1)} %bitcast.35, f32[14,1792]{1,0:T(8,128)S(1)} %bitcast.37), custom_call_target="tpu_custom_call" | custom-call | flops 1000000000 | bytes 1048576 | tf_op jit(solution)/shard_map/start/pallas_call | solution.py:452
  83.4 13.8 %all_to_all.56 = f32[128,1,128]{2,1,0:T(1,128)S(1)} all-to-all(f32[128,1,128]{2,1,0:T(1,128)S(1)} %bitcast.36), channel_id=1, replica_groups=mesh['gx_0'=4,'gx_1'=2,'gy_0'=4,'gy_1'=2,'gy_2'=2] {'gx_0','gx_1','gy_0'..., dimensions={0} | all-to-all | bytes 131072 | tf_op jit(solution)/shard_map/all_to_all | solution.py:733
  97.2 2.7 %first.1 = (f32[8,256]{1,0:T(8,128)S(1)}, f32[8,256]{1,0:T(8,128)S(1)}, f32[128,128]{1,0:T(8,128)S(1)}) custom-call(s32[2]{0:T(128)S(1)} %pad_add_fusion.place, f32[4]{0:T(128)S(1)} %add_convert_fusion.live, bf16[2,10,256,256]{3,2,1,0:T(8,128)(2,1)S(1)} %get-tuple-element.30.s_ref, f32[7,48,256]{2,1,0:T(8,128)S(1)} %get-tuple-element.40.tmap, ...), custom_call_target="tpu_custom_call" | custom-call | flops 10000000 | bytes 10485760 | tf_op jit(solution)/shard_map/first/pallas_call | solution.py:640
  100.0 13.8 %all_to_all.57 = f32[128,1,128]{2,1,0:T(1,128)S(1)} all-to-all(f32[128,1,128]{2,1,0:T(1,128)S(1)} %bitcast.34), channel_id=1, replica_groups=mesh['gx_0'=4,'gx_1'=2,'gy_0'=4,'gy_1'=2,'gy_2'=2] {'gx_0','gx_1','gy_0'..., dimensions={0} | all-to-all | bytes 131072 | tf_op jit(solution)/shard_map/all_to_all | solution.py:733
  113.8 0.8 owners.1
  114.6 0.3 copy.13
  114.9 16.0 %all_to_all.58 = f32[128,1,640]{2,1,0:T(1,128)S(1)} all-to-all(f32[128,1,640]{2,1,0:T(1,128)S(1)} %copy.13), channel_id=1, replica_groups=mesh['gx_0'=4,'gx_1'=2,'gy_0'=4,'gy_1'=2,'gy_2'=2] {'gx_0','gx_1','gy_0'..., dimensions={0} | all-to-all | bytes 655360 | tf_op jit(solution)/shard_map/all_to_all | solution.py:733
  131.0 3.7 %second.1 = (f32[8,256]{1,0:T(8,128)S(1)}, f32[8,256]{1,0:T(8,128)S(1)}, f32[8,256]{1,0:T(8,128)S(1)}, f32[8,256]{1,0:T(8,128)S(1)}, f32[128,640]{1,0:T(8,128)S(1)}) custom-call(s32[2]{0:T(128)S(1)} %pad_add_fusion.place, f32[4]{0:T(128)S(1)} %add_convert_fusion.live, bf16[2,10,256,256]{3,2,1,0:T(8,128)(2,1)S(1)} %get-tuple-element.30.s_ref, ...), custom_call_target="tpu_custom_call" | custom-call | flops 10000000 | bytes 12582912 | tf_op jit(solution)/shard_map/second/pallas_call | solution.py:685
  134.6 0.3 copy.14
  135.0 15.8 %all_to_all.59 = f32[128,1,640]{2,1,0:T(1,128)S(1)} all-to-all(f32[128,1,640]{2,1,0:T(1,128)S(1)} %copy.14), channel_id=1, replica_groups=mesh['gx_0'=4,'gx_1'=2,'gy_0'=4,'gy_1'=2,'gy_2'=2] {'gx_0','gx_1','gy_0'..., dimensions={0} | all-to-all | bytes 655360 | tf_op jit(solution)/shard_map/all_to_all | solution.py:733
  150.8 1.4 last.1
  (2 shorter events, 0.0 us)
Async XLA Ops:
  26.5 22.9 %collective-permute-start.2 = (f32[312,256]{1,0:T(8,128)}, f32[312,256]{1,0:T(8,128)S(1)}, u32[]{:S(2)}, u32[]{:S(2)}) collective-permute-start(f32[312,256]{1,0:T(8,128)} %get-tuple-element.38), channel_id=1, source_target_pairs={{0,1},{1,2},{2,3},{3,4},{4,5},{5,6},{6,7},{7,8},{8,9},{9,10},{10,1... | collective-permute-start | bytes 958472 | tf_op jit(solution)/shard_map/ppermute | solution.py:729
  31.1 18.4 %collective-permute-start.3 = (f32[312,256]{1,0:T(8,128)}, f32[312,256]{1,0:T(8,128)S(1)}, u32[]{:S(2)}, u32[]{:S(2)}) collective-permute-start(f32[312,256]{1,0:T(8,128)} %get-tuple-element.39), channel_id=1, source_target_pairs={{1,0},{2,1},{3,2},{4,3},{5,4},{6,5},{7,6},{8,7},{9,8},{10,9},{11,1... | collective-permute-start | bytes 958472 | tf_op jit(solution)/shard_map/ppermute | solution.py:729
  33.0 10.3 %collective-permute-start = (f32[160,256]{1,0:T(8,128)}, f32[160,256]{1,0:T(8,128)S(1)}, u32[]{:S(2)}, u32[]{:S(2)}) collective-permute-start(f32[160,256]{1,0:T(8,128)} %get-tuple-element.36), channel_id=1, source_target_pairs={{0,16},{16,32},{32,48},{48,64},{64,80},{80,96},{96,112},{1,17},{17... | collective-permute-start | bytes 491528 | tf_op jit(solution)/shard_map/ppermute | solution.py:729
  37.5 11.9 %collective-permute-start.1 = (f32[160,256]{1,0:T(8,128)}, f32[160,256]{1,0:T(8,128)}, u32[]{:S(2)}, u32[]{:S(2)}) collective-permute-start(f32[160,256]{1,0:T(8,128)} %get-tuple-element.37), channel_id=1, source_target_pairs={{16,0},{32,16},{48,32},{64,48},{80,64},{96,80},{112,96},{17,1},{33... | collective-permute-start | bytes 491528 | tf_op jit(solution)/shard_map/ppermute | solution.py:729
  49.4 32.4 %copy-start = (f32[1792,14]{0,1:T(8,128)S(1)}, f32[1792,14]{0,1:T(8,128)}, u32[]{:S(2)}) copy-start(f32[1792,14]{0,1:T(8,128)} %param.15) | copy-start | bytes 301060

commit v4 on v3

--- a/solution.py
+++ b/solution.py
@@ -22,7 +22,7 @@
 ONE = 160
 TWO = 312
 HALF = NF // 2
-STEPS = 3
+STEPS = 2
 CHUNK = NI // STEPS
 VC = 24
 F32 = jnp.float32
@@ -277,21 +277,24 @@
         hi, lo = split2(full)
         a_hi[m] = hi
         a_lo[m] = lo
-        size = jnp.max(jnp.sum(jnp.abs(full), axis=0, keepdims=True))
+        size = jnp.max(jnp.sum(jnp.abs(full), axis=0, keepdims=True), axis=1, keepdims=True)
         scale = 1.9 / size
         guess.append(scale)
         x[m] = scale * (2.0 * eye - scale * full)
 
+    def square_sum(left):
+        return jnp.sum(jnp.sum(left * left, axis=0, keepdims=True), axis=1, keepdims=True)
+
     def rough(state):
         count, _ = state
-        worst = jnp.float32(0.0)
+        worst = jnp.zeros((1, 1), F32)
         for m in range(7):
             now = x[m]
             near = now.astype(BF16)
             left = eye - nn(a_hi[m], near)
-            worst = jnp.maximum(worst, jnp.sum(left * left))
+            worst = jnp.maximum(worst, square_sum(left))
             x[m] = now + nn(near, left.astype(BF16))
-        return count + 1, worst
+        return count + 1, jnp.max(worst)
 
     def rough_on(state):
         count, worst = state
@@ -307,14 +310,14 @@
 
     def fine(state):
         count, _ = state
-        worst = jnp.float32(0.0)
+        worst = jnp.zeros((1, 1), F32)
         for m in range(7):
             now = x[m]
             hi, lo = split2(now)
             left = eye - (nn(a_hi[m], hi) + (nn(a_hi[m], lo) + nn(a_lo[m], hi)))
-            worst = jnp.maximum(worst, jnp.sum(left * left))
+            worst = jnp.maximum(worst, square_sum(left))
             x[m] = now + nn(hi, left.astype(BF16))
-        return count + 1, worst
+        return count + 1, jnp.max(worst)
 
     def fine_on(state):
         count, worst = state

time: 152 us -> 152 us (level)
  no operation moved by 1% of the time
where the time goes in v4:
time: 152 us
  blocking collectives  78.3 us (52%)
  Pallas kernels  48.9 us (32%)
  starting transfers between devices  12.3 us (8%)
  waiting for transfers between devices  10.4 us (7%)
    all_to_all x5, blocking collectives, exchange(): return lax.all_to_all(packet, GX_GY, 0, 0, tiled=True)  78.3 us
    pallas_call x1, Pallas kernels, schur(): pl.pallas_call(schur_kernel, grid=(2, STEPS), in_specs=[pl.BlockSpec((Non...  25.5 us
    pallas_call x1, Pallas kernels, faces(): pl.pallas_call(face_kernel, in_specs=[smem(), smem()] + [pl.BlockSpec(mem...  13.3 us
    ppermute x4, starting transfers between devices, shift(): lax.ppermute(value, axis, [(source, source + steps) for source in range(f...  12.3 us
    ppermute x4, waiting for transfers between devices, shift(): lax.ppermute(value, axis, [(source, source + steps) for source in range(f...  10.4 us
    pallas_call x1, Pallas kernels, second(): pl.pallas_call(second_kernel, in_specs=[smem(), smem()] + [vmem()] * 9, o...  3.67 us
  transfers between devices with their start and end apart: 4, of which 2 were waited for; matrix products, arithmetic and copies ran while one was open for 0% of the time, Pallas kernels for 0%

profile of v4, /device:TPU:1, one launch (start us, length us, event | category | flops | bytes accessed | tf_op | source)
XLA Modules:
  0.0 151.5 jit_solution(7126244001191356702)
XLA Ops:
  0.6 25.5 %schur.1 = (bf16[2,10,256,256]{3,2,1,0:T(8,128)(2,1)S(1)}, f32[2,288,256]{2,1,0:T(8,128)}, f32[288,256]{1,0:T(8,128)}, f32[288,256]{1,0:T(8,128)}, f32[2,288,256...) custom-call(s32[2,1,4,256]{3,2,1,0:T(4,128)} %order.1, ...), custom_call_target="tpu_custom_call" | custom-call | flops 16000000000 | bytes 33554432 | tf_op jit(solution)/shard_map/schur/pallas_call | solution.py:154
  26.2 4.6 %collective-permute-start.2 = (f32[312,256]{1,0:T(8,128)}, f32[312,256]{1,0:T(8,128)S(1)}, u32[]{:S(2)}, u32[]{:S(2)}) collective-permute-start(f32[312,256]{1,0:T(8,128)} %get-tuple-element.38), channel_id=1, source_target_pairs={{0,1},{1,2},{2,3},{3,4},{4,5},{5,6},{6,7},{7,8},{8,9},{9,10},{10,1... | collective-permute-start | bytes 958472 | tf_op jit(solution)/shard_map/ppermute | solution.py:732
  30.7 1.9 %collective-permute-start.3 = (f32[312,256]{1,0:T(8,128)}, f32[312,256]{1,0:T(8,128)S(1)}, u32[]{:S(2)}, u32[]{:S(2)}) collective-permute-start(f32[312,256]{1,0:T(8,128)} %get-tuple-element.39), channel_id=1, source_target_pairs={{1,0},{2,1},{3,2},{4,3},{5,4},{6,5},{7,6},{8,7},{9,8},{10,9},{11,1... | collective-permute-start | bytes 958472 | tf_op jit(solution)/shard_map/ppermute | solution.py:732
  32.7 4.5 %collective-permute-start = (f32[160,256]{1,0:T(8,128)}, f32[160,256]{1,0:T(8,128)S(1)}, u32[]{:S(2)}, u32[]{:S(2)}) collective-permute-start(f32[160,256]{1,0:T(8,128)} %get-tuple-element.36), channel_id=1, source_target_pairs={{0,16},{16,32},{32,48},{48,64},{64,80},{80,96},{96,112},{1,17},{17... | collective-permute-start | bytes 491528 | tf_op jit(solution)/shard_map/ppermute | solution.py:732
  37.2 1.3 collective-permute-start.1
  38.5 0.1 pad_add_fusion.place
  38.6 0.1 add_convert_fusion.live
  38.7 4.3 %collective-permute-done.q_n = f32[160,256]{1,0:T(8,128)S(1)} collective-permute-done((f32[160,256]{1,0:T(8,128)}, f32[160,256]{1,0:T(8,128)S(1)}, u32[]{:S(2)}, u32[]{:S(2)}) %collective-permute-start) | collective-permute-done | bytes 163872 | tf_op jit(solution)/shard_map/ppermute | solution.py:732
  43.0 6.1 %collective-permute-done.1.q_s = f32[160,256]{1,0:T(8,128)} collective-permute-done((f32[160,256]{1,0:T(8,128)}, f32[160,256]{1,0:T(8,128)}, u32[]{:S(2)}, u32[]{:S(2)}) %collective-permute-start.1) | collective-permute-done | bytes 163872 | tf_op jit(solution)/shard_map/ppermute | solution.py:732
  49.1 0.0 collective-permute-done.2.q_w
  49.1 0.0 collective-permute-done.3.q_e
  49.1 0.0 copy-start
  49.1 13.3 %faces.1 = (f32[7,256,256]{2,1,0:T(8,128)S(1)}, f32[7,48,256]{2,1,0:T(8,128)S(1)}, f32[8,256]{1,0:T(8,128)S(1)}, f32[8,256]{1,0:T(8,128)S(1)}, f32[24,8]{1,0:T(8,128)S(1)}, /*index=5*/f32[128,128]{1,0:T(8,128)S(1)}) custom-call(s32[2]{0:T(128)S(1)} %pad_add_fusion.place, f32[4]{0:T(128)S(1)} %add_convert_fusion.live, f32[2,288,256]{2,1,0:T(8,128)} %get-tuple-element.31.h_in, ...), custom_call_target="tpu_custom_call" | custom-call | flops 5000000000 | bytes 10485760 | tf_op jit(solution)/shard_map/faces/pallas_call | solution.py:381
  62.4 18.8 %all_to_all.55 = f32[128,1,128]{2,1,0:T(1,128)S(1)} all-to-all(f32[128,1,128]{2,1,0:T(1,128)S(1)} %bitcast.33), channel_id=1, replica_groups=mesh['gx_0'=4,'gx_1'=2,'gy_0'=4,'gy_1'=2,'gy_2'=2] {'gx_0','gx_1','gy_0'..., dimensions={0} | all-to-all | bytes 131072 | tf_op jit(solution)/shard_map/all_to_all | solution.py:736
  81.2 0.0 copy-done
  81.2 1.6 %start.1 = (f32[24,16,128]{2,1,0:T(8,128)S(1)}, f32[128,128]{1,0:T(8,128)S(1)}) custom-call(f32[128,128]{1,0:T(8,128)S(1)} %bitcast.35, f32[14,1792]{1,0:T(8,128)S(1)} %bitcast.37), custom_call_target="tpu_custom_call" | custom-call | flops 1000000000 | bytes 1048576 | tf_op jit(solution)/shard_map/start/pallas_call | solution.py:455
  82.8 13.8 %all_to_all.56 = f32[128,1,128]{2,1,0:T(1,128)S(1)} all-to-all(f32[128,1,128]{2,1,0:T(1,128)S(1)} %bitcast.36), channel_id=1, replica_groups=mesh['gx_0'=4,'gx_1'=2,'gy_0'=4,'gy_1'=2,'gy_2'=2] {'gx_0','gx_1','gy_0'..., dimensions={0} | all-to-all | bytes 131072 | tf_op jit(solution)/shard_map/all_to_all | solution.py:736
  96.6 2.7 %first.1 = (f32[8,256]{1,0:T(8,128)S(1)}, f32[8,256]{1,0:T(8,128)S(1)}, f32[128,128]{1,0:T(8,128)S(1)}) custom-call(s32[2]{0:T(128)S(1)} %pad_add_fusion.place, f32[4]{0:T(128)S(1)} %add_convert_fusion.live, bf16[2,10,256,256]{3,2,1,0:T(8,128)(2,1)S(1)} %get-tuple-element.30.s_ref, f32[7,48,256]{2,1,0:T(8,128)S(1)} %get-tuple-element.40.tmap, ...), custom_call_target="tpu_custom_call" | custom-call | flops 10000000 | bytes 10485760 | tf_op jit(solution)/shard_map/first/pallas_call | solution.py:643
  99.4 13.8 %all_to_all.57 = f32[128,1,128]{2,1,0:T(1,128)S(1)} all-to-all(f32[128,1,128]{2,1,0:T(1,128)S(1)} %bitcast.34), channel_id=1, replica_groups=mesh['gx_0'=4,'gx_1'=2,'gy_0'=4,'gy_1'=2,'gy_2'=2] {'gx_0','gx_1','gy_0'..., dimensions={0} | all-to-all | bytes 131072 | tf_op jit(solution)/shard_map/all_to_all | solution.py:736
  113.2 0.8 owners.1
  114.0 0.3 copy.13
  114.3 16.0 %all_to_all.58 = f32[128,1,640]{2,1,0:T(1,128)S(1)} all-to-all(f32[128,1,640]{2,1,0:T(1,128)S(1)} %copy.13), channel_id=1, replica_groups=mesh['gx_0'=4,'gx_1'=2,'gy_0'=4,'gy_1'=2,'gy_2'=2] {'gx_0','gx_1','gy_0'..., dimensions={0} | all-to-all | bytes 655360 | tf_op jit(solution)/shard_map/all_to_all | solution.py:736
  130.4 3.7 %second.1 = (f32[8,256]{1,0:T(8,128)S(1)}, f32[8,256]{1,0:T(8,128)S(1)}, f32[8,256]{1,0:T(8,128)S(1)}, f32[8,256]{1,0:T(8,128)S(1)}, f32[128,640]{1,0:T(8,128)S(1)}) custom-call(s32[2]{0:T(128)S(1)} %pad_add_fusion.place, f32[4]{0:T(128)S(1)} %add_convert_fusion.live, bf16[2,10,256,256]{3,2,1,0:T(8,128)(2,1)S(1)} %get-tuple-element.30.s_ref, ...), custom_call_target="tpu_custom_call" | custom-call | flops 10000000 | bytes 12582912 | tf_op jit(solution)/shard_map/second/pallas_call | solution.py:688
  134.0 0.3 copy.14
  134.4 15.8 %all_to_all.59 = f32[128,1,640]{2,1,0:T(1,128)S(1)} all-to-all(f32[128,1,640]{2,1,0:T(1,128)S(1)} %copy.14), channel_id=1, replica_groups=mesh['gx_0'=4,'gx_1'=2,'gy_0'=4,'gy_1'=2,'gy_2'=2] {'gx_0','gx_1','gy_0'..., dimensions={0} | all-to-all | bytes 655360 | tf_op jit(solution)/shard_map/all_to_all | solution.py:736
  150.2 1.4 last.1
  (2 shorter events, 0.0 us)
Async XLA Ops:
  26.2 22.9 %collective-permute-start.2 = (f32[312,256]{1,0:T(8,128)}, f32[312,256]{1,0:T(8,128)S(1)}, u32[]{:S(2)}, u32[]{:S(2)}) collective-permute-start(f32[312,256]{1,0:T(8,128)} %get-tuple-element.38), channel_id=1, source_target_pairs={{0,1},{1,2},{2,3},{3,4},{4,5},{5,6},{6,7},{7,8},{8,9},{9,10},{10,1... | collective-permute-start | bytes 958472 | tf_op jit(solution)/shard_map/ppermute | solution.py:732
  30.7 18.4 %collective-permute-start.3 = (f32[312,256]{1,0:T(8,128)}, f32[312,256]{1,0:T(8,128)S(1)}, u32[]{:S(2)}, u32[]{:S(2)}) collective-permute-start(f32[312,256]{1,0:T(8,128)} %get-tuple-element.39), channel_id=1, source_target_pairs={{1,0},{2,1},{3,2},{4,3},{5,4},{6,5},{7,6},{8,7},{9,8},{10,9},{11,1... | collective-permute-start | bytes 958472 | tf_op jit(solution)/shard_map/ppermute | solution.py:732
  32.7 10.3 %collective-permute-start = (f32[160,256]{1,0:T(8,128)}, f32[160,256]{1,0:T(8,128)S(1)}, u32[]{:S(2)}, u32[]{:S(2)}) collective-permute-start(f32[160,256]{1,0:T(8,128)} %get-tuple-element.36), channel_id=1, source_target_pairs={{0,16},{16,32},{32,48},{48,64},{64,80},{80,96},{96,112},{1,17},{17... | collective-permute-start | bytes 491528 | tf_op jit(solution)/shard_map/ppermute | solution.py:732
  37.2 11.9 %collective-permute-start.1 = (f32[160,256]{1,0:T(8,128)}, f32[160,256]{1,0:T(8,128)}, u32[]{:S(2)}, u32[]{:S(2)}) collective-permute-start(f32[160,256]{1,0:T(8,128)} %get-tuple-element.37), channel_id=1, source_target_pairs={{16,0},{32,16},{48,32},{64,48},{80,64},{96,80},{112,96},{17,1},{33... | collective-permute-start | bytes 491528 | tf_op jit(solution)/shard_map/ppermute | solution.py:732
  49.1 32.1 %copy-start = (f32[1792,14]{0,1:T(8,128)S(1)}, f32[1792,14]{0,1:T(8,128)}, u32[]{:S(2)}) copy-start(f32[1792,14]{0,1:T(8,128)} %param.15) | copy-start | bytes 301060
